TPU v7x, 32 devices: a whole 2x2x4 slice. The times are simulated.
32 devices in a mesh: dp: 8 (over z, x), seq: 4 (over y, core).
Axes of the slice: x: 2, y: 2, z: 4, core: 2. Of those that a mesh axis runs over, the one named last changes fastest.
Arguments:
- tokens: bfloat16 [8, 3072, 768], P('dp', 'seq'), may hold values from -6 to 6
- w_qkv: bfloat16 [768, 2304], P('dp'), may hold values from -0.21875 to 0.21875
- bias_query: bfloat16 [768], P('dp'), may hold values from -1.25 to 1.25
- bias_value: bfloat16 [768], P('dp'), may hold values from -0.3125 to 0.3125
- w_attn_out: bfloat16 [768, 768], P('dp'), may hold values from -3.5 to 3.5
- bias_attn_out: bfloat16 [768], P('dp'), may hold values from -0.625 to 0.625
- norm1_gain: bfloat16 [768], P('dp'), may hold values from 0.5 to 1.5
- norm1_shift: bfloat16 [768], P('dp'), may hold values from -0.625 to 0.625
- w_up: bfloat16 [768, 3072], P('dp'), may hold values from -0.21875 to 0.21875
- bias_up: bfloat16 [3072], P('dp'), may hold values from -0.625 to 0.625
- w_down: bfloat16 [3072, 768], P('dp'), may hold values from -0.109375 to 0.109375
- bias_down: bfloat16 [768], P('dp'), may hold values from -0.625 to 0.625
- norm2_gain: bfloat16 [768], P('dp'), may hold values from 0.5 to 1.5
- norm2_shift: bfloat16 [768], P('dp'), may hold values from -0.625 to 0.625
- w_proj: bfloat16 [768, 128], P('dp'), may hold values from -0.01953125 to 0.01953125
- doc_ids: int32 [8, 3072], P('dp'), may hold values from 0 to 7, never falling along the last dimension, each value on 1 to 1152 neighbouring positions
- cotangent: bfloat16 [8, 3072, 128], P('dp', 'seq'), may hold values from -6 to 6
Outputs:
- embeddings: float32 [8, 3072, 128], P('dp', 'seq')
- grad_tokens: float32 [8, 3072, 768], P('dp', 'seq')
- grad_w_qkv: float32 [768, 2304], P('dp')
- grad_bias_query: float32 [768], P('dp')
- grad_bias_value: float32 [768], P('dp')
- grad_w_attn_out: float32 [768, 768], P('dp')
- grad_bias_attn_out: float32 [768], P('dp')
- grad_norm1_gain: float32 [768], P('dp')
- grad_norm1_shift: float32 [768], P('dp')
- grad_w_up: float32 [768, 3072], P('dp')
- grad_bias_up: float32 [3072], P('dp')
- grad_w_down: float32 [3072, 768], P('dp')
- grad_bias_down: float32 [768], P('dp')
- grad_norm2_gain: float32 [768], P('dp')
- grad_norm2_shift: float32 [768], P('dp')
- grad_w_proj: float32 [768, 128], P('dp')
Inputs may be any that keep to these rules, and one draw needn't show every extreme that they name: doc_ids never falls along a stream; every one of the 8 documents has 1 to 1152 tokens, and one has exactly 1152.
All inputs are finite; a program needn't handle non-finite values.
Results may differ from a plain program's by a relative error of at most 0.02.
Values may be sent and summed in bfloat16 or wider, within the bound.
No kernel may reach another device: no remote copies, remote signals or barrier semaphores. Data moves between devices by JAX's collectives and lax.ppermute only.
A program may use at most 192 MiB of HBM per device.

v0:
```python
from functools import partial

import jax
import jax.numpy as jnp
from jax import lax
from jax.sharding import PartitionSpec as P

D = 768
H = 12
HD = 64
QBLOCK = 512


NORM_EPS = 1e-12
UNIT_EPS = 1e-06
MASK_FILL = -1000000000.0


def layer_norm(resid, gain, shift):
    center = resid - jnp.mean(resid, axis=-1, keepdims=True)
    spread = jnp.mean(center * center, axis=-1, keepdims=True)
    return center * lax.rsqrt(spread + NORM_EPS) * gain + shift


def unit_rows(projected):
    return projected * lax.rsqrt(jnp.sum(projected * projected, axis=-1, keepdims=True) + UNIT_EPS)


def product(left, right):
    return jnp.dot(left, right, preferred_element_type=jnp.float32)


def lead_dot(left, right):
    return lax.dot_general(
        left, right, (((0,), (0,)), ((), ())), preferred_element_type=jnp.float32
    )


def tail_dot(left, right):
    return lax.dot_general(
        left, right, (((1,), (1,)), ((), ())), preferred_element_type=jnp.float32
    )


def split_heads(qkv_heads):
    length = qkv_heads.shape[0]
    arranged = qkv_heads.reshape(length, -1, 3, HD).transpose(1, 2, 0, 3)
    return (arranged[:, 0], arranged[:, 1], arranged[:, 2])


def block_scores(query_block, doc_block, key_rows, doc_row, scale):
    scores = (
        jnp.einsum("hqe,hke->hqk", query_block, key_rows, preferred_element_type=jnp.float32)
        * scale
    )
    same_doc = doc_block[:, None] == doc_row[None, :]
    return jnp.where(same_doc[None], scores, MASK_FILL)


def attend_forward(qkv_heads, doc_row, scale):
    query_rows, key_rows, value_rows = split_heads(qkv_heads)
    heads_dev = query_rows.shape[0]
    length = query_rows.shape[1]
    block_rows = min(QBLOCK, length)
    context = jnp.zeros((heads_dev, length, HD), jnp.bfloat16)
    log_total = jnp.zeros((heads_dev, length), jnp.float32)

    def one_block(index, state):
        context, log_total = state
        start = index * block_rows
        query_block = lax.dynamic_slice_in_dim(query_rows, start, block_rows, 1)
        doc_block = lax.dynamic_slice_in_dim(doc_row, start, block_rows, 0)
        scores = block_scores(query_block, doc_block, key_rows, doc_row, scale)
        row_max = jnp.max(scores, axis=-1, keepdims=True)
        row_total = row_max + jnp.log(jnp.sum(jnp.exp(scores - row_max), axis=-1, keepdims=True))
        attn_probs = jnp.exp(scores - row_total).astype(jnp.bfloat16)
        mixed = jnp.einsum(
            "hqk,hke->hqe", attn_probs, value_rows, preferred_element_type=jnp.float32
        )
        context = lax.dynamic_update_slice_in_dim(context, mixed.astype(jnp.bfloat16), start, 1)
        log_total = lax.dynamic_update_slice_in_dim(log_total, row_total[..., 0], start, 1)
        return (context, log_total)

    context, log_total = lax.fori_loop(0, length // block_rows, one_block, (context, log_total))
    return (context.transpose(1, 0, 2).reshape(length, -1), log_total)


def attend_backward(qkv_heads, log_total, d_context_heads, doc_row, scale):
    query_rows, key_rows, value_rows = split_heads(qkv_heads)
    heads_dev = query_rows.shape[0]
    length = query_rows.shape[1]
    d_output = d_context_heads.reshape(length, heads_dev, HD).transpose(1, 0, 2)
    block_rows = min(QBLOCK, length)
    d_query = jnp.zeros((heads_dev, length, HD), jnp.bfloat16)
    d_key = jnp.zeros((heads_dev, length, HD), jnp.float32)
    d_value = jnp.zeros((heads_dev, length, HD), jnp.float32)

    def one_block(index, state):
        d_query, d_key, d_value = state
        start = index * block_rows
        query_block = lax.dynamic_slice_in_dim(query_rows, start, block_rows, 1)
        doc_block = lax.dynamic_slice_in_dim(doc_row, start, block_rows, 0)
        output_block = lax.dynamic_slice_in_dim(d_output, start, block_rows, 1)
        total_block = lax.dynamic_slice_in_dim(log_total, start, block_rows, 1)
        scores = block_scores(query_block, doc_block, key_rows, doc_row, scale)
        probs_full = jnp.exp(scores - total_block[..., None])
        probs_low = probs_full.astype(jnp.bfloat16)
        d_weights = jnp.einsum(
            "hqe,hke->hqk", output_block, value_rows, preferred_element_type=jnp.float32
        )
        inner = jnp.sum(probs_full * d_weights, axis=-1, keepdims=True)
        d_scores = (scale * probs_full * (d_weights - inner)).astype(jnp.bfloat16)
        query_grad = jnp.einsum(
            "hqk,hke->hqe", d_scores, key_rows, preferred_element_type=jnp.float32
        )
        d_query = lax.dynamic_update_slice_in_dim(
            d_query, query_grad.astype(jnp.bfloat16), start, 1
        )
        d_key = d_key + jnp.einsum(
            "hqk,hqe->hke", d_scores, query_block, preferred_element_type=jnp.float32
        )
        d_value = d_value + jnp.einsum(
            "hqk,hqe->hke", probs_low, output_block, preferred_element_type=jnp.float32
        )
        return (d_query, d_key, d_value)

    d_query, d_key, d_value = lax.fori_loop(
        0, length // block_rows, one_block, (d_query, d_key, d_value)
    )
    stacked = jnp.stack([d_query, d_key.astype(jnp.bfloat16), d_value.astype(jnp.bfloat16)], axis=2)
    return stacked.transpose(1, 0, 2, 3).reshape(length, -1)


def sum_grads(item_one, item_two, item_three, item_four, item_five, item_six, item_seven):
    part_one, part_two, part_three, part_four, part_five, part_six, part_seven = (
        lax.psum_scatter(
            item_one.astype(jnp.bfloat16), "dp", scatter_dimension=0, tiled=True
        ).astype(jnp.float32),
        lax.psum_scatter(
            item_two.astype(jnp.bfloat16), "dp", scatter_dimension=0, tiled=True
        ).astype(jnp.float32),
        lax.psum_scatter(
            item_three.astype(jnp.bfloat16), "dp", scatter_dimension=0, tiled=True
        ).astype(jnp.float32),
        lax.psum_scatter(
            item_four.astype(jnp.bfloat16), "dp", scatter_dimension=0, tiled=True
        ).astype(jnp.float32),
        lax.psum_scatter(
            item_five.astype(jnp.bfloat16), "dp", scatter_dimension=0, tiled=True
        ).astype(jnp.float32),
        lax.psum_scatter(
            item_six.astype(jnp.bfloat16), "dp", scatter_dimension=0, tiled=True
        ).astype(jnp.float32),
        lax.psum_scatter(
            item_seven.astype(jnp.bfloat16), "dp", scatter_dimension=0, tiled=True
        ).astype(jnp.float32),
    )
    return (
        lax.psum(part_one.astype(jnp.bfloat16), "seq").astype(jnp.float32),
        lax.psum(part_two.astype(jnp.bfloat16), "seq").astype(jnp.float32),
        lax.psum(part_three.astype(jnp.bfloat16), "seq").astype(jnp.float32),
        lax.psum(part_four.astype(jnp.bfloat16), "seq").astype(jnp.float32),
        lax.psum(part_five.astype(jnp.bfloat16), "seq").astype(jnp.float32),
        lax.psum(part_six.astype(jnp.bfloat16), "seq").astype(jnp.float32),
        lax.psum(part_seven.astype(jnp.bfloat16), "seq").astype(jnp.float32),
    )


def shards(
    tokens,
    w_qkv,
    bias_query,
    bias_value,
    w_attn_out,
    bias_attn_out,
    norm1_gain,
    norm1_shift,
    w_up,
    bias_up,
    w_down,
    bias_down,
    norm2_gain,
    norm2_shift,
    w_proj,
    doc_ids,
    cotangent,
):
    gathered = (
        lax.all_gather(w_qkv, "dp", axis=0, tiled=True),
        lax.all_gather(bias_query, "dp", axis=0, tiled=True),
        lax.all_gather(bias_value, "dp", axis=0, tiled=True),
        lax.all_gather(w_attn_out, "dp", axis=0, tiled=True),
        lax.all_gather(bias_attn_out, "dp", axis=0, tiled=True),
        lax.all_gather(norm1_gain, "dp", axis=0, tiled=True),
        lax.all_gather(norm1_shift, "dp", axis=0, tiled=True),
        lax.all_gather(w_up, "dp", axis=0, tiled=True),
        lax.all_gather(bias_up, "dp", axis=0, tiled=True),
        lax.all_gather(w_down, "dp", axis=0, tiled=True),
        lax.all_gather(bias_down, "dp", axis=0, tiled=True),
        lax.all_gather(norm2_gain, "dp", axis=0, tiled=True),
        lax.all_gather(norm2_shift, "dp", axis=0, tiled=True),
        lax.all_gather(w_proj, "dp", axis=0, tiled=True),
    )
    (
        full_qkv,
        full_query_bias,
        full_value_bias,
        full_attn_out,
        full_attn_bias,
        gain_first,
        shift_first,
        full_up,
        full_up_bias,
        full_down,
        full_down_bias,
        gain_second,
        shift_second,
        full_proj,
    ) = gathered
    scale = HD ** (-0.5)
    token_rows = tokens[0]
    doc_row = doc_ids[0]
    empty_bias = jnp.zeros((H, 1, HD), jnp.float32)
    qkv_bias = jnp.concatenate(
        [
            full_query_bias.astype(jnp.float32).reshape(H, 1, HD),
            empty_bias,
            full_value_bias.astype(jnp.float32).reshape(H, 1, HD),
        ],
        axis=1,
    ).reshape(1, 3 * D)
    qkv = (product(token_rows, full_qkv) + qkv_bias).astype(jnp.bfloat16)
    qkv_heads = lax.all_to_all(qkv, "seq", split_axis=1, concat_axis=0, tiled=True)
    context_heads, log_total = attend_forward(qkv_heads, doc_row, scale)
    context = lax.all_to_all(context_heads, "seq", split_axis=0, concat_axis=1, tiled=True)
    attn = product(context, full_attn_out) + full_attn_bias.astype(jnp.float32)
    resid_first = token_rows.astype(jnp.float32) + attn
    hidden_first, norm_first_pull = jax.vjp(
        layer_norm, resid_first, gain_first.astype(jnp.float32), shift_first.astype(jnp.float32)
    )
    hidden_first_low = hidden_first.astype(jnp.bfloat16)
    pre = product(hidden_first_low, full_up) + full_up_bias.astype(jnp.float32)
    act, gelu_pull = jax.vjp(partial(jax.nn.gelu, approximate=False), pre)
    act_low = act.astype(jnp.bfloat16)
    ffn = product(act_low, full_down) + full_down_bias.astype(jnp.float32)
    resid_second = hidden_first + ffn
    hidden_second, norm_second_pull = jax.vjp(
        layer_norm, resid_second, gain_second.astype(jnp.float32), shift_second.astype(jnp.float32)
    )
    hidden_second_low = hidden_second.astype(jnp.bfloat16)
    projected = product(hidden_second_low, full_proj)
    embed, unit_pull = jax.vjp(unit_rows, projected)
    back_qkv, back_attn_out, back_up, back_down, back_proj = (
        lax.all_gather(w_qkv, "dp", axis=0, tiled=True),
        lax.all_gather(w_attn_out, "dp", axis=0, tiled=True),
        lax.all_gather(w_up, "dp", axis=0, tiled=True),
        lax.all_gather(w_down, "dp", axis=0, tiled=True),
        lax.all_gather(w_proj, "dp", axis=0, tiled=True),
    )
    (d_projected,) = unit_pull(cotangent[0].astype(jnp.float32))
    d_projected_low = d_projected.astype(jnp.bfloat16)
    grad_proj = lead_dot(hidden_second_low, d_projected_low)
    d_hidden_second = tail_dot(d_projected_low, back_proj)
    d_resid_second, grad_gain_second, grad_shift_second = norm_second_pull(d_hidden_second)
    d_ffn = d_resid_second.astype(jnp.bfloat16)
    grad_down = lead_dot(act_low, d_ffn)
    grad_down_bias = jnp.sum(d_ffn.astype(jnp.float32), axis=0)
    (d_pre,) = gelu_pull(tail_dot(d_ffn, back_down))
    d_pre_low = d_pre.astype(jnp.bfloat16)
    grad_up = lead_dot(hidden_first_low, d_pre_low)
    grad_up_bias = jnp.sum(d_pre_low.astype(jnp.float32), axis=0)
    late_sums = sum_grads(
        grad_proj,
        grad_gain_second,
        grad_shift_second,
        grad_down,
        grad_down_bias,
        grad_up,
        grad_up_bias,
    )
    d_hidden_first = d_resid_second + tail_dot(d_pre_low, back_up)
    d_resid_first, grad_gain_first, grad_shift_first = norm_first_pull(d_hidden_first)
    d_attn = d_resid_first.astype(jnp.bfloat16)
    grad_attn_out = lead_dot(context, d_attn)
    grad_attn_bias = jnp.sum(d_attn.astype(jnp.float32), axis=0)
    d_context = tail_dot(d_attn, back_attn_out).astype(jnp.bfloat16)
    d_context_heads = lax.all_to_all(d_context, "seq", split_axis=1, concat_axis=0, tiled=True)
    d_qkv_heads = attend_backward(qkv_heads, log_total, d_context_heads, doc_row, scale)
    d_qkv = lax.all_to_all(d_qkv_heads, "seq", split_axis=0, concat_axis=1, tiled=True)
    grad_qkv = lead_dot(token_rows, d_qkv)
    column_sums = jnp.sum(d_qkv.astype(jnp.float32), axis=0).reshape(H, 3, HD)
    grad_query_bias = column_sums[:, 0].reshape(D)
    grad_value_bias = column_sums[:, 2].reshape(D)
    grad_input = d_resid_first + tail_dot(d_qkv, back_qkv)
    early_sums = sum_grads(
        grad_gain_first,
        grad_shift_first,
        grad_attn_out,
        grad_attn_bias,
        grad_qkv,
        grad_query_bias,
        grad_value_bias,
    )
    return (
        embed[None],
        grad_input[None],
        early_sums[4],
        early_sums[5],
        early_sums[6],
        early_sums[2],
        early_sums[3],
        early_sums[0],
        early_sums[1],
        late_sums[5],
        late_sums[6],
        late_sums[3],
        late_sums[4],
        late_sums[1],
        late_sums[2],
        late_sums[0],
    )


def solution(mesh):
    in_specs = (
        P("dp", "seq", None),
        P("dp", None),
        P("dp"),
        P("dp"),
        P("dp", None),
        P("dp"),
        P("dp"),
        P("dp"),
        P("dp", None),
        P("dp"),
        P("dp", None),
        P("dp"),
        P("dp"),
        P("dp"),
        P("dp", None),
        P("dp", None),
        P("dp", "seq", None),
    )
    out_specs = (
        P("dp", "seq", None),
        P("dp", "seq", None),
        P("dp", None),
        P("dp"),
        P("dp"),
        P("dp", None),
        P("dp"),
        P("dp"),
        P("dp"),
        P("dp", None),
        P("dp"),
        P("dp", None),
        P("dp"),
        P("dp"),
        P("dp"),
        P("dp", None),
    )
    return jax.shard_map(shards, mesh=mesh, in_specs=in_specs, out_specs=out_specs, check_vma=False)
```

profile of v0, /device:TPU:0, one launch (start us, length us, event | category | flops | bytes accessed | tf_op | source)
XLA Modules:
  0.0 1306.8 jit_solution(6482969643006698503)
XLA Ops:
  18.1 41.2 %all-reduce.18 = (bf16[768]{0:T(1024)(128)(2,1)S(1)}, bf16[768]{0:T(1024)(128)(2,1)S(1)}, bf16[768]{0:T(1024)(128)(2,1)}, bf16[768]{0:T(1024)(128)(2,1)}, bf16[7...) all-reduce(bf16[768]{0:T(1024)(128)(2,1)S(1)} %dynamic-update-slice, ...), channel_id=1, replica_groups=mesh['dp'=8,'seq'=4] {'dp'}, use_global_device_ids=true, to_apply=%add.1 | all-reduce | flops 6144 | bytes 24576
  59.7 18.4 %all-gather.6.cloned.1.call-done = bf16[768,2304]{1,0:T(8,128)(2,1)} async-done(((bf16[96,2304]{1,0:T(8,128)(2,1)}), bf16[768,2304]{1,0:T(8,128)(2,1)}) %all-gather.6.cloned.1.call-update) | async-done | bytes 3538960 | tf_op jit(solution)/shard_map/all_gather | solution.py:189
  91.2 40.5 %all-to-all-done = bf16[768,4,576]{0,2,1:T(8,128)(2,1)S(1)} async-done(((bf16[768,4,576]{0,2,1:T(8,128)(2,1)}), bf16[768,4,576]{0,2,1:T(8,128)(2,1)S(1)}, u32[]{:S(2)}, u32[]{:S(2)}) %all-to-all-start) | async-done | bytes 3538976 | tf_op jit(solution)/shard_map/all_to_all | solution.py:233
  145.3 112.6 %while.33 = (s32[]{:T(128)}, bf16[3,3072,64]{1,2,0:T(8,128)(2,1)}, f32[3,3072]{1,0:T(4,128)S(1)}, s32[3072]{0:T(1024)S(1)}, s32[1,3072]{1,0:T(1,128)S(1)}, /*ind...) while((s32[]{:T(128)}, bf16[3,3072,64]{1,2,0:T(8,128)(2,1)}, ...), condition=%wide.region_3.4_spmd, body=%wide.region_0.3_spmd.sunk | while | flops 1261533696 | bytes 65743024 | solution.py:84
  267.1 26.4 %all-gather = bf16[8,1,384]{2,1,0:T(2,128)(2,1)S(1)} all-gather(bf16[1,1,384]{2,1,0:T(2,128)(2,1)S(1)} %reshape.276), channel_id=1, replica_groups=mesh['dp'=8,'seq'=4] {'dp'}, dimensions={0}, use_global_device_ids=true | all-gather | bytes 6912 | tf_op jit(solution)/shard_map/all_gather | solution.py:197
  293.6 31.1 %all_gather.60 = bf16[768,128]{1,0:T(8,128)(2,1)S(1)} all-gather(bf16[96,128]{1,0:T(8,128)(2,1)S(1)} %copy-done.19), channel_id=1, replica_groups=mesh['dp'=8,'seq'=4] {'dp'}, dimensions={0}, use_global_device_ids=true | all-gather | bytes 221184 | tf_op jit(solution)/shard_map/all_gather | solution.py:202
  329.3 29.3 %multiply_convert_fusion.1 = (bf16[768,3072]{1,0:T(8,128)(2,1)}, f32[768,3072]{1,0:T(8,128)}, f32[768,3072]{1,0:T(8,128)}) fusion(f32[3072]{0:T(1024)S(1)} %bitcast.133, bf16[768,3072]{1,0:T(8,128)(2,1)} %all-gather.10.cloned.1.call-done, f32[768,768]{0,1:T(8,128)S(1)} %get-tuple-element.553, f32[768]{0:T(1024)S(1)} %convert_element_type.222, ...), kind=kOutput, calls=%fused_computation.43 | convolution fusion | flops 3782541312 | bytes 30695424 | tf_op jit(solution)/shard_map/dot_general | solution.py:30
  407.7 15.7 %all-to-all-done.2 = bf16[768,4,192]{0,2,1:T(8,128)(2,1)S(1)} async-done(((bf16[768,4,192]{0,2,1:T(8,128)(2,1)}), bf16[768,4,192]{0,2,1:T(8,128)(2,1)S(1)}, u32[]{:S(2)}, u32[]{:S(2)}) %all-to-all-start.2) | async-done | bytes 1179680 | tf_op jit(solution)/shard_map/all_to_all | solution.py:287
  430.0 340.7 %while.34 = (s32[]{:T(128)}, bf16[3,3072,64]{1,2,0:T(8,128)(2,1)}, f32[3,3072,64]{1,2,0:T(8,128)}, f32[3,3072,64]{1,2,0:T(8,128)}, s32[3072]{0:T(1024)S(1)}, /*i...) while((s32[]{:T(128)}, bf16[3,3072,64]{1,2,0:T(8,128)(2,1)}, ...), condition=%wide.region_16.17_spmd.clone, body=%wide.region_14.0_spmd.clone.sunk | while | flops 3099425280 | bytes 237367536 | solution.py:127
  449.4 14.3 %multiply_reduce_fusion.9 = (f32[3,512]{1,0:T(4,128)S(1)}, f32[3,512,3072]{2,1,0:T(8,128)}) fusion(f32[3,512,3072]{2,1,0:T(8,128)} %copy-done, f32[3,512]{1,0:T(4,128)S(1)} %constant_dynamic-slice_fusion.2, pred[512,3072]{1,0:T(8,128)(4,1)S(1)} %broadcast_compare_fusion.5, bf16[3,3072,64]{1,2,0:T(8,128)(2,1)} %get-tuple-element.767, ...), kind=kOutput, calls=%fused_computation.17.clone.1 | convolution fusion | flops 627571200 | bytes 40710148 | tf_op jit(solution)/shard_map/while/body/eval_jaxpr/hqe,hke->hqk/dot_general | solution.py:108
  463.7 14.1 %multiply_convert_fusion.3 = bf16[3,512,3072]{2,1,0:T(8,128)(2,1)S(1)} fusion(f32[3,512,3072]{2,1,0:T(8,128)} %get-tuple-element.689, f32[3,512,3072]{2,1,0:T(8,128)} %copy-done, f32[3,512]{1,0:T(4,128)S(1)} %get-tuple-element.690, f32[3,512]{1,0:T(4,128)S(1)} %constant_dynamic-slice_fusion.2, pred[512,3072]{1,0:T(8,128)(4,1)S(1)} %broadcast_compare_fusion.5), kind=kLoop, calls=%fused_computation.16.clone.1 | loop fusion | flops 33030144 | bytes 48771072 | tf_op jit(solution)/shard_map/while/body/eval_jaxpr/convert_element_type | solution.py:112
  505.5 14.3 %multiply_reduce_fusion.9 = (f32[3,512]{1,0:T(4,128)S(1)}, f32[3,512,3072]{2,1,0:T(8,128)}) fusion(f32[3,512,3072]{2,1,0:T(8,128)} %copy-done, f32[3,512]{1,0:T(4,128)S(1)} %constant_dynamic-slice_fusion.2, pred[512,3072]{1,0:T(8,128)(4,1)S(1)} %broadcast_compare_fusion.5, bf16[3,3072,64]{1,2,0:T(8,128)(2,1)} %get-tuple-element.767, ...), kind=kOutput, calls=%fused_computation.17.clone.1 | convolution fusion | flops 627571200 | bytes 40710148 | tf_op jit(solution)/shard_map/while/body/eval_jaxpr/hqe,hke->hqk/dot_general | solution.py:108
  562.5 14.3 %multiply_reduce_fusion.9 = (f32[3,512]{1,0:T(4,128)S(1)}, f32[3,512,3072]{2,1,0:T(8,128)}) fusion(f32[3,512,3072]{2,1,0:T(8,128)} %copy-done, f32[3,512]{1,0:T(4,128)S(1)} %constant_dynamic-slice_fusion.2, pred[512,3072]{1,0:T(8,128)(4,1)S(1)} %broadcast_compare_fusion.5, bf16[3,3072,64]{1,2,0:T(8,128)(2,1)} %get-tuple-element.767, ...), kind=kOutput, calls=%fused_computation.17.clone.1 | convolution fusion | flops 627571200 | bytes 40710148 | tf_op jit(solution)/shard_map/while/body/eval_jaxpr/hqe,hke->hqk/dot_general | solution.py:108
  619.4 14.3 %multiply_reduce_fusion.9 = (f32[3,512]{1,0:T(4,128)S(1)}, f32[3,512,3072]{2,1,0:T(8,128)}) fusion(f32[3,512,3072]{2,1,0:T(8,128)} %copy-done, f32[3,512]{1,0:T(4,128)S(1)} %constant_dynamic-slice_fusion.2, pred[512,3072]{1,0:T(8,128)(4,1)S(1)} %broadcast_compare_fusion.5, bf16[3,3072,64]{1,2,0:T(8,128)(2,1)} %get-tuple-element.767, ...), kind=kOutput, calls=%fused_computation.17.clone.1 | convolution fusion | flops 627571200 | bytes 40710148 | tf_op jit(solution)/shard_map/while/body/eval_jaxpr/hqe,hke->hqk/dot_general | solution.py:108
  676.4 14.3 %multiply_reduce_fusion.9 = (f32[3,512]{1,0:T(4,128)S(1)}, f32[3,512,3072]{2,1,0:T(8,128)}) fusion(f32[3,512,3072]{2,1,0:T(8,128)} %copy-done, f32[3,512]{1,0:T(4,128)S(1)} %constant_dynamic-slice_fusion.2, pred[512,3072]{1,0:T(8,128)(4,1)S(1)} %broadcast_compare_fusion.5, bf16[3,3072,64]{1,2,0:T(8,128)(2,1)} %get-tuple-element.767, ...), kind=kOutput, calls=%fused_computation.17.clone.1 | convolution fusion | flops 627571200 | bytes 40710148 | tf_op jit(solution)/shard_map/while/body/eval_jaxpr/hqe,hke->hqk/dot_general | solution.py:108
  733.4 14.3 %multiply_reduce_fusion.9 = (f32[3,512]{1,0:T(4,128)S(1)}, f32[3,512,3072]{2,1,0:T(8,128)}) fusion(f32[3,512,3072]{2,1,0:T(8,128)} %copy-done, f32[3,512]{1,0:T(4,128)S(1)} %constant_dynamic-slice_fusion.2, pred[512,3072]{1,0:T(8,128)(4,1)S(1)} %broadcast_compare_fusion.5, bf16[3,3072,64]{1,2,0:T(8,128)(2,1)} %get-tuple-element.767, ...), kind=kOutput, calls=%fused_computation.17.clone.1 | convolution fusion | flops 627571200 | bytes 40710148 | tf_op jit(solution)/shard_map/while/body/eval_jaxpr/hqe,hke->hqk/dot_general | solution.py:108
  781.0 43.8 %all_to_all.70 = bf16[4,768,576]{1,2,0:T(8,128)(2,1)S(1)} all-to-all(bf16[4,768,576]{1,2,0:T(8,128)(2,1)S(1)} %copy.81), channel_id=1, replica_groups=mesh['dp'=8,'seq'=4] {'seq'}, dimensions={0} | all-to-all | bytes 7077888 | tf_op jit(solution)/shard_map/all_to_all | solution.py:289
  862.9 47.9 %reduce-scatter.16.cloned.1.call-done = bf16[96,2304]{1,0:T(8,128)(2,1)} async-done(((bf16[768,2304]{1,0:T(8,128)(2,1)}), bf16[96,2304]{1,0:T(8,128)(2,1)}) %reduce-scatter.16.cloned.1.call-update) | async-done | bytes 442384
  912.9 66.0 %reduce-scatter.8.cloned.1.call-done = bf16[96,768]{1,0:T(8,128)(2,1)} async-done(((bf16[768,768]{1,0:T(8,128)(2,1)}), bf16[96,768]{1,0:T(8,128)(2,1)}) %reduce-scatter.8.cloned.1.call-update) | async-done | bytes 147472 | tf_op jit(solution)/shard_map/reduce_scatter | solution.py:142
  978.9 98.4 %reduce-scatter.10.cloned.1.call-done = bf16[96,3072]{1,0:T(8,128)(2,1)} async-done(((bf16[768,3072]{1,0:T(8,128)(2,1)}), bf16[96,3072]{1,0:T(8,128)(2,1)}) %reduce-scatter.10.cloned.1.call-update) | async-done | bytes 589840 | tf_op jit(solution)/shard_map/reduce_scatter | solution.py:151
  1077.3 99.0 %reduce-scatter.12.cloned.1.call-done = bf16[384,768]{1,0:T(8,128)(2,1)} async-done(((bf16[3072,768]{1,0:T(8,128)(2,1)}), bf16[384,768]{1,0:T(8,128)(2,1)}) %reduce-scatter.12.cloned.1.call-update) | async-done | bytes 589840 | tf_op jit(solution)/shard_map/reduce_scatter | solution.py:145
  1187.3 36.5 %all-reduce.17 = (bf16[768]{0:T(1024)(128)(2,1)S(1)}, bf16[768]{0:T(1024)(128)(2,1)S(1)}, bf16[768]{0:T(1024)(128)(2,1)S(1)}, bf16[768]{0:T(1024)(128)(2,1)S(1)}...) all-reduce(bf16[768]{0:T(1024)(128)(2,1)S(1)} %convert_element_type, ...), channel_id=3, replica_groups=mesh['dp'=8,'seq'=4] {'dp'}, use_global_device_ids=true, to_apply=%region_20.21.clone | all-reduce | flops 9216 | bytes 36864
  1224.5 17.3 %reduce-scatter.14.cloned.1.call-done = bf16[96,128]{1,0:T(8,128)(2,1)} async-done(((bf16[768,128]{1,0:T(8,128)(2,1)}), bf16[96,128]{1,0:T(8,128)(2,1)}) %reduce-scatter.14.cloned.1.call-update) | async-done | bytes 24592 | tf_op jit(solution)/shard_map/reduce_scatter | solution.py:136
  1257.9 34.7 %all-reduce.23.cloned.1.call-done = (bf16[96,2304]{0,1:T(8,128)(2,1)}, bf16[96,768]{1,0:T(8,128)(2,1)}, bf16[96,3072]{1,0:T(8,128)(2,1)}, bf16[384,768]{1,0:T(8,128)(2,1)}) async-done(((bf16[96,2304]{0,1:T(8,128)(2,1)}, bf16[96,768]{1,0:T(8,128)(2,1)}, bf16[96,3072]{1,0:T(8,128)(2,1)}, bf16[384,768]{1,0:T(8,128)(2,1)}), (bf16[96,2304]{0,1:T(8,128)(2,1)}, bf16[96,768]{1,0:T(8,128)(2,1)}, ...) | async-done | bytes 1769488 | tf_op jit(solution)/shard_map/psum | solution.py:163
  (319 shorter events, 542.7 us)
Async XLA Ops:
  7.2 70.9 %all-gather.6.cloned.1.call-start = ((), (), s32[]{:S(2)}) async-start(), calls=%async_computation.9 | async-start | bytes 3981312 | tf_op jit(solution)/shard_map/all_gather | solution.py:189
  7.9 316.8 %all-gather.8.cloned.1.call-start = ((), (), s32[]{:S(2)}) async-start(), calls=%async_computation.10 | async-start | bytes 1327104 | tf_op jit(solution)/shard_map/all_gather | solution.py:192
  8.7 320.6 %all-gather.10.cloned.1.call-start = ((), (), s32[]{:S(2)}) async-start(), calls=%async_computation.11 | async-start | bytes 5308416 | tf_op jit(solution)/shard_map/all_gather | solution.py:196
  86.9 44.8 %all-to-all-start = ((bf16[768,4,576]{0,2,1:T(8,128)(2,1)}), bf16[768,4,576]{0,2,1:T(8,128)(2,1)S(1)}, u32[]{:S(2)}, u32[]{:S(2)}) async-start(bf16[768,4,576]{0,2,1:T(8,128)(2,1)} %bitcast.117), calls=%async_computation | async-start | bytes 7077888 | tf_op jit(solution)/shard_map/all_to_all | solution.py:233
  90.6 268.0 %all-gather.12.cloned.1.call-start = ((), (), s32[]{:S(2)}) async-start(), calls=%async_computation.12 | async-start | bytes 5308416 | tf_op jit(solution)/shard_map/all_gather | solution.py:198
  261.8 31.7 %copy-start.16 = (bf16[1,768,128]{2,1,0:T(8,128)(2,1)S(1)}, bf16[1,768,128]{2,1,0:T(8,128)(2,1)}, u32[]{:S(2)}) copy-start(bf16[1,768,128]{2,1,0:T(8,128)(2,1)} %param.37) | copy-start | bytes 589828
  261.8 31.9 %copy-start.19 = (bf16[96,128]{1,0:T(8,128)(2,1)S(1)}, bf16[96,128]{1,0:T(8,128)(2,1)}, u32[]{:S(2)}) copy-start(bf16[96,128]{1,0:T(8,128)(2,1)} %param.35) | copy-start | bytes 73732
  261.8 63.0 %all-to-all-start.1 = ((bf16[4,768,192]{1,2,0:T(8,128)(2,1)}), bf16[4,768,192]{1,2,0:T(8,128)(2,1)S(1)}, u32[]{:S(2)}, u32[]{:S(2)}) async-start(bf16[4,768,192]{1,2,0:T(8,128)(2,1)} %copy.75), calls=%async_computation.1 | async-start | bytes 2359296 | tf_op jit(solution)/shard_map/all_to_all | solution.py:235
  266.9 132.1 %copy-start.20 = (f32[768]{0:T(1024)}, f32[768]{0:T(1024)S(1)}, u32[]{:S(2)}) copy-start(f32[768]{0:T(1024)S(1)} %convert_element_type.221) | copy-start | bytes 9220
  267.0 91.7 %copy-start.28 = (f32[768]{0:T(1024)}, f32[768]{0:T(1024)S(1)}, u32[]{:S(2)}) copy-start(f32[768]{0:T(1024)S(1)} %convert_element_type.222) | copy-start | bytes 9220
  328.9 29.7 %copy-start.4 = (f32[768,768]{0,1:T(8,128)}, f32[768,768]{0,1:T(8,128)S(1)}, u32[]{:S(2)}) copy-start(f32[768,768]{0,1:T(8,128)S(1)} %get-tuple-element.553) | copy-start | bytes 7077892
  329.0 70.1 %copy-start.17 = (f32[768]{0:T(1024)}, f32[768]{0:T(1024)S(1)}, u32[]{:S(2)}) copy-start(f32[768]{0:T(1024)S(1)} %broadcast_multiply_fusion.1) | copy-start | bytes 9220
  329.3 69.8 %copy-start.22 = (f32[768]{0:T(1024)}, f32[768]{0:T(1024)S(1)}, u32[]{:S(2)}) copy-start(f32[768]{0:T(1024)S(1)} %fusion.42) | copy-start | bytes 9220
  379.4 14.4 %slice-start = ((s8[4718592]{0:T(1024)(128)(4,1)}), s8[4194304]{0:T(1024)(128)(4,1)S(1)}, s32[]{:S(2)}) async-start(s8[4718592]{0:T(1024)(128)(4,1)} %bitcast.135), calls=%async_computation.19 | async-start | bytes 8388608
  380.3 13.6 %slice-start.1 = ((s8[4718592]{0:T(1024)(128)(4,1)}), s8[524288]{0:T(1024)(128)(4,1)S(1)}, s32[]{:S(2)}) async-start(s8[4718592]{0:T(1024)(128)(4,1)} %bitcast.135), calls=%async_computation.20 | async-start | bytes 1048576
  404.1 19.3 %all-to-all-start.2 = ((bf16[768,4,192]{0,2,1:T(8,128)(2,1)}), bf16[768,4,192]{0,2,1:T(8,128)(2,1)S(1)}, u32[]{:S(2)}, u32[]{:S(2)}) async-start(bf16[768,4,192]{0,2,1:T(8,128)(2,1)} %bitcast.17), calls=%async_computation.2 | async-start | bytes 2359296 | tf_op jit(solution)/shard_map/all_to_all | solution.py:287
  407.6 503.2 %reduce-scatter.16.cloned.1.call-start = ((), (), s32[]{:S(2)}) async-start(), calls=%async_computation.17 | async-start | bytes 3981312
  781.0 43.8 %copy-start.11 = (bf16[1,768,768]{2,1,0:T(8,128)(2,1)S(1)}, bf16[1,768,768]{2,1,0:T(8,128)(2,1)}, u32[]{:S(2)}) copy-start(bf16[1,768,768]{2,1,0:T(8,128)(2,1)} %param.21) | copy-start | bytes 3538948
  834.9 144.0 %reduce-scatter.8.cloned.1.call-start = ((), (), s32[]{:S(2)}) async-start(), calls=%async_computation.13 | async-start | bytes 1327104 | tf_op jit(solution)/shard_map/reduce_scatter | solution.py:142
  838.8 238.5 %reduce-scatter.10.cloned.1.call-start = ((), (), s32[]{:S(2)}) async-start(), calls=%async_computation.14 | async-start | bytes 5308416 | tf_op jit(solution)/shard_map/reduce_scatter | solution.py:151
  848.0 328.3 %reduce-scatter.12.cloned.1.call-start = ((), (), s32[]{:S(2)}) async-start(), calls=%async_computation.15 | async-start | bytes 5308416 | tf_op jit(solution)/shard_map/reduce_scatter | solution.py:145
  856.9 384.8 %reduce-scatter.14.cloned.1.call-start = ((), (), s32[]{:S(2)}) async-start(), calls=%async_computation.16 | async-start | bytes 221184 | tf_op jit(solution)/shard_map/reduce_scatter | solution.py:136
  859.4 316.9 %copy-start.25 = (f32[768]{0:T(1024)S(1)}, f32[768]{0:T(1024)}, u32[]{:S(2)}) copy-start(f32[768]{0:T(1024)} %copy-done.24) | copy-start | bytes 9220
  859.5 433.1 %all-reduce.23.cloned.1.call-start = ((), (), s32[]{:S(2)}) async-start(), calls=%async_computation.18 | async-start | bytes 3833856 | tf_op jit(solution)/shard_map/psum | solution.py:163
  (35 other events, 170.4 us)
Sparse Core Ops, SparseCore 0:
  10.2 67.8 all-gather.5
  80.2 39.8 all-gather.7
  122.4 78.0 all-gather.9
  202.4 77.7 all-gather.11
  835.0 75.7 reduce-scatter.15
  914.6 64.2 reduce-scatter.7
  982.5 94.7 reduce-scatter.9
  1080.9 95.3 reduce-scatter.11
  1180.1 61.5 reduce-scatter.13
  1244.8 47.7 all-reduce.22
where the time goes:
time: 1310 us
  waiting for transfers between devices  440 us (34%)
  matrix products  392 us (30%)
  blocking collectives  190 us (15%)
  other arithmetic  149 us (11%)
  local copies, waits for them, and re-layouts  106 us (8%)
  between operations  17.1 us (1%)
    reduce_scatter x1, waiting for transfers between devices, sum_grads(): lax.psum_scatter(item_four.astype(jnp.bfloat16), 'dp', scatter_dimension=...  99 us
    reduce_scatter x1, waiting for transfers between devices, sum_grads(): lax.psum_scatter(item_six.astype(jnp.bfloat16), 'dp', scatter_dimension=0...  98.4 us
    dot_general x6, matrix products, one_block(): jnp.einsum('hqe,hke->hqk', output_block, value_rows, preferred_element_ty...  86 us
    convert_element_type x6, other arithmetic, one_block(): d_scores = (scale * probs_full * (d_weights - inner)).astype(jnp.bfloat16)  84.3 us
    unnamed x2, blocking collectives  77.7 us
    reduce_scatter x1, waiting for transfers between devices, sum_grads(): lax.psum_scatter(item_three.astype(jnp.bfloat16), 'dp', scatter_dimension...  66 us
    dot_general x12, matrix products, block_scores(): jnp.einsum('hqe,hke->hqk', query_block, key_rows, preferred_element_type=...  53.3 us
    dot_general x6, matrix products, one_block(): jnp.einsum('hqk,hqe->hke', probs_low, output_block, preferred_element_typ...  51.7 us
  transfers between devices with their start and end apart: 13, of which 9 were waited for; matrix products, arithmetic and copies ran while one was open for 17% of the time, Pallas kernels for 0%

commit v1 on v0

v1 whole, which is shorter than its diff:
```python
import jax, jax.numpy as jnp
from jax import lax
from jax.experimental import pallas as pl
from jax.experimental.pallas import tpu as pltpu

HD = 64
BLK = 256
LANES = 256
DOC_LANE = 192
STAT_LANE = 200
FAR = 2.0 ** 30
NT = (((1,), (1,)), ((), ()))
TN = (((0,), (0,)), ((), ()))
f32, bf16 = jnp.float32, jnp.bfloat16


def lane_of(shape):
    return lax.broadcasted_iota(jnp.int32, shape, 1)


def three_terms(x, lane):
    top = x.astype(bf16).astype(f32)
    mid = (x - top).astype(bf16).astype(f32)
    rest = x - top - mid
    return jnp.where(lane == STAT_LANE, top, jnp.where(lane == STAT_LANE + 1, mid, rest))


def is_stat(lane):
    return (lane >= STAT_LANE) & (lane < STAT_LANE + 3)


def own_lanes(lane, h):
    return (lane >= h * HD) & (lane < h * HD + HD)


def project_kernel(x_ref, w_ref, b_ref, doc_ref, q_ref, k_ref, v_ref):
    x = x_ref[...]
    lane = lane_of((x.shape[0], LANES))
    hot = lane - DOC_LANE == doc_ref[...]
    docs = (lane >= DOC_LANE) & (lane < STAT_LANE)
    def part(j):
        y = jnp.dot(x, w_ref[:, j * LANES:(j + 1) * LANES], preferred_element_type=f32)
        return (y + b_ref[:, j * LANES:(j + 1) * LANES]).astype(bf16)
    q = part(0).astype(f32) * (HD ** -0.5)
    q_ref[...] = jnp.where(hot, -FAR, q).astype(bf16)
    one = jnp.where(docs & ~hot | is_stat(lane), 1.0, part(1).astype(f32))
    k_ref[...] = one.astype(bf16)
    v_ref[...] = jnp.where(is_stat(lane), 1.0, part(2).astype(f32)).astype(bf16)


def forward_kernel(lo_ref, hi_ref, q_ref, k_ref, v_ref, ctx_ref, qa_ref, vm, scr, acc, qm, peak):
    heads = 3
    qb = pl.program_id(0)
    lane = lane_of((BLK, LANES))

    @pl.when(qb == 0)
    def _():
        def fill(i, _):
            rows = pl.ds(i * BLK, BLK)
            v = v_ref[rows, :].astype(f32)
            for h in range(heads):
                vm[h, rows, :] = jnp.where(own_lanes(lane, h), v, jnp.where(lane == DOC_LANE + h, 1.0, 0.0)).astype(bf16)
            return 0
        lax.fori_loop(0, v_ref.shape[0] // BLK, fill, 0)

    lo, hi = lo_ref[qb], hi_ref[qb]
    q = q_ref[...].astype(f32)
    acc[...] = jnp.zeros_like(acc)
    masked = [jnp.where(own_lanes(lane, h) | (lane >= DOC_LANE), q, 0.0) for h in range(heads)]
    for h in range(heads):
        qm[h] = masked[h].astype(bf16)
        peak[h] = jnp.full((BLK, 128), -jnp.inf, f32)

    def score(kb, _):
        keys = k_ref[pl.ds(kb * BLK, BLK), :]
        for h in range(heads):
            s = lax.dot_general(qm[h], keys, NT, preferred_element_type=f32)
            scr[h, kb - lo] = s
            peak[h] = jnp.maximum(peak[h], jnp.maximum(s[:, :128], s[:, 128:]))
        return 0
    lax.fori_loop(lo, hi, score, 0)
    tops = [jnp.max(peak[h], axis=1, keepdims=True) for h in range(heads)]
    for h in range(heads):
        peak[h] = jnp.broadcast_to(tops[h], (BLK, 128))

    def mix(kb, _):
        parts = []
        for h in range(heads):
            top = peak[h]
            s = scr[h, kb - lo]
            p = jnp.exp(s - jnp.concatenate([top, top], axis=1)).astype(bf16)
            parts.append(jnp.dot(p, vm[h, pl.ds(kb * BLK, BLK), :], preferred_element_type=f32))
        acc[...] += parts[0] + parts[1] + parts[2]
        return 0
    lax.fori_loop(lo, hi, mix, 0)
    out = acc[...]
    totals = [out[:, DOC_LANE + h:DOC_LANE + h + 1] for h in range(heads)]
    inv = jnp.where(lane < HD, 1.0 / totals[0], jnp.where(lane < 2 * HD, 1.0 / totals[1], 1.0 / totals[2]))
    ctx_ref[...] = (out * inv).astype(bf16)[:, :heads * HD]
    for h in range(heads):
        lse = tops[h] + jnp.log(totals[h])
        qa_ref[h] = jnp.where(is_stat(lane), three_terms(-lse + jnp.zeros((BLK, LANES), f32), lane), masked[h]).astype(bf16)


def backward_kernel(lo_ref, hi_ref, qa_ref, k_ref, v_ref, o_ref, do_ref, dq_ref, dkv_ref, km, dm, dqs, dks, dvs):
    heads = 3
    kb = pl.program_id(0)
    length = k_ref.shape[0]
    lane = lane_of((BLK, LANES))

    @pl.when(kb == 0)
    def _():
        row = lax.broadcasted_iota(jnp.int32, (heads * HD, LANES), 0)
        col = lane_of((heads * HD, LANES))

        def fill(i, _):
            rows = pl.ds(i * BLK, BLK)
            k = k_ref[rows, :].astype(f32)
            do = do_ref[rows, :].astype(f32)
            prod = do * o_ref[rows, :].astype(f32)
            top = prod.astype(bf16)
            rest = (prod - top.astype(f32)).astype(bf16)
            do = jnp.concatenate([do, jnp.zeros((BLK, LANES - heads * HD), f32)], axis=1)
            for h in range(heads):
                pick = jnp.where((row >= h * HD) & (row < h * HD + HD) & is_stat(col), -1.0, 0.0).astype(bf16)
                inner = jnp.dot(top, pick, preferred_element_type=f32) + jnp.dot(rest, pick, preferred_element_type=f32)
                km[h, rows, :] = jnp.where(own_lanes(lane, h), k, 0.0).astype(bf16)
                dm[h, rows, :] = jnp.where(is_stat(lane), three_terms(inner, lane), jnp.where(own_lanes(lane, h), do, 0.0)).astype(bf16)
            dqs[rows, :] = jnp.zeros((BLK, LANES), f32)
            return 0
        lax.fori_loop(0, length // BLK, fill, 0)

    dks[...] = jnp.zeros_like(dks)
    dvs[...] = jnp.zeros_like(dvs)
    here = pl.ds(kb * BLK, BLK)
    k = k_ref[here, :]
    v = v_ref[here, :]

    def pair(qb, _):
        rows = pl.ds(qb * BLK, BLK)
        dsl, dkl, dvl = [], [], []
        for h in range(heads):
            qa = qa_ref[h, rows, :]
            da = dm[h, rows, :]
            p = jnp.exp(lax.dot_general(k, qa, NT, preferred_element_type=f32))
            dp = lax.dot_general(v, da, NT, preferred_element_type=f32)
            ds = (p * dp).astype(bf16)
            dvl.append(jnp.dot(p.astype(bf16), da, preferred_element_type=f32))
            dkl.append(jnp.dot(ds, qa, preferred_element_type=f32))
            dsl.append(lax.dot_general(ds, km[h, here, :], TN, preferred_element_type=f32))
        dvs[...] += dvl[0] + dvl[1] + dvl[2]
        dks[...] += dkl[0] + dkl[1] + dkl[2]
        dqs[rows, :] += dsl[0] + dsl[1] + dsl[2]
        return 0
    lax.fori_loop(lo_ref[kb], hi_ref[kb], pair, 0)
    keep = lane < heads * HD
    dkv_ref[:, :LANES] = jnp.where(keep, dks[...], 0.0).astype(bf16)
    dkv_ref[:, LANES:] = jnp.where(keep, dvs[...], 0.0).astype(bf16)

    @pl.when(kb == pl.num_programs(0) - 1)
    def _():
        def drain(i, _):
            rows = pl.ds(i * BLK, BLK)
            dq_ref[rows, :] = (dqs[rows, :] * (HD ** -0.5)).astype(bf16)
            return 0
        lax.fori_loop(0, length // BLK, drain, 0)


VM = 60 * 1024 * 1024


def params():
    return pltpu.CompilerParams(dimension_semantics=("arbitrary",), vmem_limit_bytes=VM)


def whole(shape):
    return pl.BlockSpec(shape, lambda i, *_: (0,) * len(shape))


def project(x, w, b, doc):
    length = x.shape[0]
    spec = pl.BlockSpec((BLK, LANES), lambda i: (i, 0))
    return pl.pallas_call(
        project_kernel, grid=(length // BLK,),
        in_specs=[pl.BlockSpec((BLK, x.shape[1]), lambda i: (i, 0)), whole(w.shape), whole(b.shape), pl.BlockSpec((BLK, 1), lambda i: (i, 0))],
        out_specs=[spec] * 3, out_shape=[jax.ShapeDtypeStruct((length, LANES), bf16)] * 3,
        compiler_params=params(), name="project")(x, w, b, doc)


def attend_forward(lo, hi, q, k, v):
    length = q.shape[0]
    return pl.pallas_call(
        forward_kernel,
        grid_spec=pltpu.PrefetchScalarGridSpec(
            num_scalar_prefetch=2, grid=(length // BLK,),
            in_specs=[pl.BlockSpec((BLK, LANES), lambda i, *_: (i, 0)), whole((length, LANES)), whole((length, LANES))],
            out_specs=[pl.BlockSpec((BLK, 3 * HD), lambda i, *_: (i, 0)), pl.BlockSpec((3, BLK, LANES), lambda i, *_: (0, i, 0))],
            scratch_shapes=[pltpu.VMEM((3, length, LANES), bf16), pltpu.VMEM((3, length // BLK, BLK, BLK), f32), pltpu.VMEM((BLK, LANES), f32),
                            pltpu.VMEM((3, BLK, LANES), bf16), pltpu.VMEM((3, BLK, 128), f32)]),
        out_shape=[jax.ShapeDtypeStruct((length, 3 * HD), bf16), jax.ShapeDtypeStruct((3, length, LANES), bf16)],
        compiler_params=params(), name="attend_forward")(lo, hi, q, k, v)


def attend_backward(lo, hi, qa, k, v, o, do):
    length = k.shape[0]
    return pl.pallas_call(
        backward_kernel,
        grid_spec=pltpu.PrefetchScalarGridSpec(
            num_scalar_prefetch=2, grid=(length // BLK,),
            in_specs=[whole((3, length, LANES)), whole((length, LANES)), whole((length, LANES)), whole((length, 3 * HD)), whole((length, 3 * HD))],
            out_specs=[whole((length, LANES)), pl.BlockSpec((BLK, 2 * LANES), lambda i, *_: (i, 0))],
            scratch_shapes=[pltpu.VMEM((3, length, LANES), bf16), pltpu.VMEM((3, length, LANES), bf16), pltpu.VMEM((length, LANES), f32),
                            pltpu.VMEM((BLK, LANES), f32), pltpu.VMEM((BLK, LANES), f32)]),
        out_shape=[jax.ShapeDtypeStruct((length, LANES), bf16), jax.ShapeDtypeStruct((length, 2 * LANES), bf16)],
        compiler_params=params(), name="attend_backward")(lo, hi, qa, k, v, o, do)


def block_ranges(doc_row):
    length = doc_row.shape[0]
    first = doc_row[::BLK]
    last = doc_row[BLK - 1::BLK]
    begin = jnp.sum((doc_row[None, :] < first[:, None]).astype(jnp.int32), axis=1)
    end = jnp.sum((doc_row[None, :] <= last[:, None]).astype(jnp.int32), axis=1)
    return begin // BLK, (end + BLK - 1) // BLK


from functools import partial

from jax.sharding import PartitionSpec as P

D = 768
H = 12
FF = 3072
EMB = 128
HEADS = 3
NORM_EPS = 1e-12
UNIT_EPS = 1e-06


def layer_norm(resid, gain, shift):
    center = resid - jnp.mean(resid, axis=-1, keepdims=True)
    spread = jnp.mean(center * center, axis=-1, keepdims=True)
    return center * lax.rsqrt(spread + NORM_EPS) * gain + shift


def unit_rows(projected):
    return projected * lax.rsqrt(jnp.sum(projected * projected, axis=-1, keepdims=True) + UNIT_EPS)


def product(left, right):
    return jnp.dot(left, right, preferred_element_type=f32)


def lead_dot(left, right):
    return lax.dot_general(left, right, TN, preferred_element_type=f32)


def tail_dot(left, right):
    return lax.dot_general(left, right, NT, preferred_element_type=f32)


def swap(x, axis, mask, size):
    return lax.ppermute(x, axis, [(i, i ^ mask) for i in range(size)])


def masks(size):
    out = []
    m = 1
    while m < size:
        out.append(m)
        m *= 2
    return out


def pick(x, index, axis=0):
    return lax.dynamic_index_in_dim(x, index, axis, keepdims=False)


def gather_dp(x, n):
    held = x[None]
    for m in reversed(masks(n)):
        held = jnp.concatenate([held, swap(held, "dp", m, n)], axis=0)
    return held


def order_of(n):
    seen = [0]
    for m in reversed(masks(n)):
        seen = seen + [k ^ m for k in seen]
    return {k: at for at, k in enumerate(seen)}


def gathered_rows(own, n, i):
    place = order_of(n)
    table = jnp.asarray([place[k] for k in range(n)], jnp.int32)
    return [pick(own, table[j ^ i]) for j in range(n)]


def halves_kernel(block_ref, c_ref, own_ref, other_ref, out_ref):
    c = c_ref[0]
    width = own_ref.shape[2]

    @pl.when(c == 0)
    def _():
        out_ref[0, :, :width] = own_ref[0]
        out_ref[0, :, width:] = other_ref[0]

    @pl.when(c != 0)
    def _():
        out_ref[0, :, :width] = other_ref[0]
        out_ref[0, :, width:] = own_ref[0]


def join_halves(own, other, n, i, c):
    rows, width = own.shape[1:]
    place = order_of(n)
    table = jnp.asarray([place[k] for k in range(n)], jnp.int32)
    blocks = table[jnp.arange(n, dtype=jnp.int32) ^ i]
    spec = pl.BlockSpec((1, rows, width), lambda j, b, c: (b[j], 0, 0))
    return pl.pallas_call(
        halves_kernel,
        grid_spec=pltpu.PrefetchScalarGridSpec(
            num_scalar_prefetch=2, grid=(n,), in_specs=[spec, spec],
            out_specs=pl.BlockSpec((1, rows, 2 * width), lambda j, b, c: (j, 0, 0))),
        out_shape=jax.ShapeDtypeStruct((n, rows, 2 * width), own.dtype),
        compiler_params=params(), name="join_halves")(blocks, c.reshape(1), own, other)


def ordered(pieces, s, axis):
    size = pieces[0].shape[axis]
    shape = list(pieces[0].shape)
    shape[axis] = size * len(pieces)
    out = jnp.zeros(shape, pieces[0].dtype)
    for k, piece in enumerate(pieces):
        out = lax.dynamic_update_slice_in_dim(out, piece, (s ^ k) * size, axis)
    return out


def core_reduce(full, c):
    width = full.shape[-1] // 2
    mine = lax.dynamic_slice_in_dim(full, c * width, width, full.ndim - 1)
    theirs = lax.dynamic_slice_in_dim(full, (1 - c) * width, width, full.ndim - 1)
    got = swap(theirs.astype(bf16), "seq", 1, 4)
    return (mine.astype(f32) + got.astype(f32)).astype(bf16)


def scatter_dp(part, n, i):
    held = part
    for m in masks(n):
        bit = (i // m) % 2
        held = held.reshape((held.shape[0] // 2, 2) + held.shape[1:])
        keep = pick(held, bit, 1)
        got = swap(pick(held, 1 - bit, 1), "dp", m, n)
        held = (keep.astype(f32) + got.astype(f32)).astype(bf16)
    return held[0]


def share_seq(held, c):
    got = swap(held, "seq", 2, 4)
    total = (held.astype(f32) + got.astype(f32)).astype(bf16)
    other = swap(total, "seq", 1, 4)
    first = jnp.where(c == 0, total, other)
    second = jnp.where(c == 0, other, total)
    return jnp.concatenate([first, second], axis=-1).astype(f32)


def shards(
    n,
    tokens,
    w_qkv,
    bias_query,
    bias_value,
    w_attn_out,
    bias_attn_out,
    norm1_gain,
    norm1_shift,
    w_up,
    bias_up,
    w_down,
    bias_down,
    norm2_gain,
    norm2_shift,
    w_proj,
    doc_ids,
    cotangent,
):
    s = lax.axis_index("seq")
    i = lax.axis_index("dp")
    c = s % 2
    own = D // n
    token_rows = tokens[0]
    doc_row = doc_ids[0]
    far = swap(token_rows, "seq", 2, 4)
    near = swap(token_rows, "seq", 1, 4)
    opposite = swap(far, "seq", 1, 4)
    pieces = [token_rows, near, far, opposite]
    mine = lax.dynamic_slice_in_dim(w_qkv, s * HEADS * 3 * HD, HEADS * 3 * HD, 1)
    mine = mine.reshape(own, HEADS, 3, HD).transpose(0, 2, 1, 3).reshape(own, 3, HEADS * HD)
    mine = jnp.pad(mine, ((0, 0), (0, 0), (0, LANES - HEADS * HD))).reshape(own, 3 * LANES)
    vectors = [bias_query, bias_value, bias_attn_out, norm1_gain, norm1_shift, bias_down, norm2_gain, norm2_shift]
    short = jnp.concatenate(vectors + [bias_up]).reshape(1, -1)
    width = short.shape[1]
    short = jnp.pad(short, ((0, 0), (0, -width % D))).reshape(-1, D)
    extra = short.shape[0]
    early = gather_dp(jnp.concatenate([mine, short], axis=0), n)
    blocks = gathered_rows(early, n, i)
    heads_qkv = jnp.concatenate([b[:own] for b in blocks], axis=0)
    flat = jnp.stack([b[own:].reshape(extra * D)[:width] for b in blocks])
    vecs = [flat[:, k * own:(k + 1) * own].reshape(D).astype(f32) for k in range(8)]
    full_query_bias, full_value_bias, full_attn_bias, gain_first, shift_first, full_down_bias, gain_second, shift_second = vecs
    full_up_bias = flat[:, 8 * own:].reshape(FF).astype(f32)
    def half(x):
        return lax.dynamic_slice_in_dim(x, c * (D // 2), D // 2, 1)
    up_rows = jnp.concatenate([w_up[:, k * D:(k + 1) * D] for k in range(FF // D)], axis=0)
    proj_rows = w_proj.reshape(-1, D)
    bundle_a = half(jnp.concatenate([up_rows, w_attn_out, proj_rows], axis=0))
    bundle_b = half(w_down)
    own_a = gather_dp(bundle_a, n)
    own_b = gather_dp(bundle_b, n)
    other_a = swap(own_a, "seq", 1, 4)
    other_b = swap(own_b, "seq", 1, 4)
    joined_a = join_halves(own_a, other_a, n, i, c)
    full_down = join_halves(own_b, other_b, n, i, c).reshape(FF, D)
    count = FF // D
    full_up = [joined_a[:, k * own:(k + 1) * own].reshape(D, D) for k in range(count)]
    full_up = jnp.concatenate(full_up, axis=1)
    full_attn_out = joined_a[:, count * own:(count + 1) * own].reshape(D, D)
    full_proj = joined_a[:, (count + 1) * own:].reshape(D, EMB)
    lo, hi = block_ranges(doc_row)
    at = s * HEADS * HD
    gap = jnp.zeros((LANES - HEADS * HD,), f32)
    bias_row = jnp.concatenate([
        lax.dynamic_slice_in_dim(full_query_bias, at, HEADS * HD, 0), gap, jnp.zeros((LANES,), f32),
        lax.dynamic_slice_in_dim(full_value_bias, at, HEADS * HD, 0), gap]).reshape(1, 3 * LANES)
    all_tokens = ordered(pieces, s, 0)
    q, k, v = project(all_tokens, heads_qkv, bias_row, doc_row.reshape(-1, 1))
    context_heads, qa = attend_forward(lo, hi, q, k, v)
    length = token_rows.shape[0]
    def rows_of(x, j):
        return lax.dynamic_slice_in_dim(x, j * length, length, 0)
    got = [rows_of(context_heads, s)] + [swap(rows_of(context_heads, s ^ m), "seq", m, 4) for m in (1, 2, 3)]
    context = ordered(got, s, 1)
    attn = product(context, full_attn_out) + full_attn_bias
    resid_first = token_rows.astype(f32) + attn
    hidden_first, norm_first_pull = jax.vjp(layer_norm, resid_first, gain_first, shift_first)
    hidden_first_low = hidden_first.astype(bf16)
    pre = product(hidden_first_low, full_up) + full_up_bias
    act, gelu_pull = jax.vjp(partial(jax.nn.gelu, approximate=False), pre)
    act_low = act.astype(bf16)
    ffn = product(act_low, full_down) + full_down_bias
    resid_second = hidden_first + ffn
    hidden_second, norm_second_pull = jax.vjp(layer_norm, resid_second, gain_second, shift_second)
    hidden_second_low = hidden_second.astype(bf16)
    projected = product(hidden_second_low, full_proj)
    embed, unit_pull = jax.vjp(unit_rows, projected)
    (d_projected,) = unit_pull(cotangent[0].astype(f32))
    d_projected_low = d_projected.astype(bf16)
    grad_proj = lead_dot(hidden_second_low, d_projected_low)
    d_hidden_second = tail_dot(d_projected_low, full_proj)
    d_resid_second, grad_gain_second, grad_shift_second = norm_second_pull(d_hidden_second)
    d_ffn = d_resid_second.astype(bf16)
    grad_down = lead_dot(act_low, d_ffn).astype(bf16)
    grad_down_bias = jnp.sum(d_ffn.astype(f32), axis=0)
    (d_pre,) = gelu_pull(tail_dot(d_ffn, full_down))
    d_pre_low = d_pre.astype(bf16)
    grad_up = lead_dot(hidden_first_low, d_pre_low).astype(bf16)
    grad_up_bias = jnp.sum(d_pre_low.astype(f32), axis=0)
    d_hidden_first = d_resid_second + tail_dot(d_pre_low, full_up)
    d_resid_first, grad_gain_first, grad_shift_first = norm_first_pull(d_hidden_first)
    d_attn = d_resid_first.astype(bf16)
    out_rows = full_attn_out.reshape(4, HEADS * HD, D)
    d_context = [tail_dot(d_attn, pick(out_rows, s ^ m)).astype(bf16) for m in range(4)]
    d_got = [d_context[0]] + [swap(d_context[m], "seq", m, 4) for m in (1, 2, 3)]
    d_context_heads = ordered(d_got, s, 0)
    grad_attn_out = lead_dot(context, d_attn).astype(bf16)
    grad_attn_bias = jnp.sum(d_attn.astype(f32), axis=0)
    dq, dkv = attend_backward(lo, hi, qa, k, v, context_heads, d_context_heads)
    sum_down = share_seq(scatter_dp(core_reduce(grad_down.reshape(n, FF // n, D), c), n, i), c)
    sum_up = share_seq(scatter_dp(core_reduce(grad_up.reshape(n, own, FF), c), n, i), c)
    shorts = [grad_attn_bias, grad_gain_first, grad_shift_first, grad_down_bias, grad_gain_second, grad_shift_second]
    shorts = jnp.concatenate([g.reshape(n, own) for g in shorts] + [grad_up_bias.reshape(n, FF // n)], axis=1)
    wide = shorts.shape[1]
    shorts = jnp.pad(shorts, ((0, 0), (0, -wide % D))).astype(bf16).reshape(n, -1, D)
    rest = jnp.concatenate([grad_attn_out.reshape(n, own, D), grad_proj.astype(bf16).reshape(n, -1, D), shorts], axis=1)
    sum_rest = share_seq(scatter_dp(core_reduce(rest, c), n, i), c)
    proj_count = own * EMB // D
    sum_attn_out = sum_rest[:own]
    sum_proj = sum_rest[own:own + proj_count].reshape(own, EMB)
    sums = sum_rest[own + proj_count:].reshape(-1)
    d_qkv = jnp.concatenate([dq, dkv], axis=1)
    shares = tail_dot(d_qkv, heads_qkv).astype(bf16).reshape(2, 2, length, D)
    mine_share = pick(shares, c, 1)
    got_share = swap(pick(shares, 1 - c, 1), "seq", 1, 4)
    pair = (mine_share.astype(f32) + got_share.astype(f32)).astype(bf16)
    y = s // 2
    from_far = swap(pick(pair, 1 - y), "seq", 2, 4)
    grad_input = d_resid_first + pick(pair, y).astype(f32) + from_far.astype(f32)
    grad_qkv = lead_dot(all_tokens, d_qkv).astype(bf16)
    column_sums = jnp.sum(d_qkv.astype(f32), axis=0)
    def spread(x):
        return lax.dynamic_update_slice_in_dim(jnp.zeros((D,), f32), x, at, 0).reshape(n, own)
    sides = jnp.concatenate([spread(column_sums[:HEADS * HD]), spread(column_sums[2 * LANES:2 * LANES + HEADS * HD])], axis=1)
    sides = jnp.pad(sides, ((0, 0), (0, D - 2 * own))).astype(bf16).reshape(n, 1, D)
    tail = scatter_dp(jnp.concatenate([grad_qkv.reshape(n, own, D), sides], axis=1), n, i)
    two = jnp.stack([tail, swap(tail, "seq", 2, 4)])
    two_more = swap(two, "seq", 1, 4)
    stacked = jnp.stack([two[0], two_more[0], two[1], two_more[1]])
    parts = [pick(stacked, s ^ j) for j in range(4)]
    def natural(x):
        return x[:own].reshape(own, 3, LANES)[:, :, :HEADS * HD].reshape(own, 3, HEADS, HD).transpose(0, 2, 1, 3).reshape(own, -1)
    sum_qkv = jnp.concatenate([natural(x) for x in parts], axis=1).astype(f32)
    side_sum = sum(x[own].astype(f32) for x in parts)
    return (
        embed[None],
        grad_input[None],
        sum_qkv,
        side_sum[:own],
        side_sum[own:2 * own],
        sum_attn_out,
        sums[:own],
        sums[own:2 * own],
        sums[2 * own:3 * own],
        sum_up,
        sums[6 * own:6 * own + FF // n],
        sum_down,
        sums[3 * own:4 * own],
        sums[4 * own:5 * own],
        sums[5 * own:6 * own],
        sum_proj,
    )


def solution(mesh):
    rows, line, stream = P("dp", None), P("dp"), P("dp", "seq", None)
    in_specs = (stream, rows, line, line, rows, line, line, line, rows, line, rows, line, line, line, rows, rows, stream)
    out_specs = (stream, stream, rows, line, line, rows, line, line, line, rows, line, rows, line, line, line, rows)
    return jax.shard_map(partial(shards, mesh.shape["dp"]), mesh=mesh, in_specs=in_specs, out_specs=out_specs, check_vma=False)
```

time: 1310 us -> 672 us (0.51)
  matrix products: 392 us -> 102 us
  waiting for transfers between devices: 440 us -> 170 us
  blocking collectives: 190 us -> 0 us
  Pallas kernels: 0 us -> 156 us
  other arithmetic: 149 us -> 45.9 us
  starting transfers between devices: 11.8 us -> 42.2 us
  local copies, waits for them, and re-layouts: 106 us -> 130 us
    dot_general x57 -> x17, matrix products: 392 us -> 102 us  [the longest x4 41 us: product(): return jnp.dot(left, right, preferred_element_type=f32)]
    reduce_scatter x4 -> x0, waiting for transfers between devices: 281 us -> none  [the longest x1 99 us: sum_grads(): lax.psum_scatter(item_four.astype(jnp.bfloat16), 'dp', scatter_dimension=...]
    ppermute x0 -> x45, waiting for transfers between devices: none -> 170 us  [swap(): return lax.ppermute(x, axis, [(i, i ^ mask) for i in range(size)])]
    pallas_call x0 -> x5, Pallas kernels: none -> 156 us  [the longest x1 80.6 us: attend_backward(): pl.pallas_call(backward_kernel, grid_spec=pltpu.PrefetchScalarGridSpec(nu...]
    unnamed x2 -> x0, blocking collectives: 77.7 us -> none
    convert_element_type x28 -> x24, other arithmetic: 95.8 us -> 18.5 us  [the longest x3 7.31 us: core_reduce(): return (mine.astype(f32) + got.astype(f32)).astype(bf16)]
    all_gather x2 -> x0, blocking collectives: 57.5 us -> none  [the longest x1 31.1 us: shards(): lax.all_gather(w_proj, 'dp', axis=0, tiled=True)]
    all_to_all x3 -> x0, waiting for transfers between devices: 56.2 us -> none  [the longest x1 40.5 us: shards(): lax.all_to_all(qkv, 'seq', split_axis=1, concat_axis=0, tiled=True)]
  transfers between devices with their start and end apart: 13 -> 45, of which waited for: 9 -> 20; matrix products, arithmetic and copies ran while one was open for 17% -> 22% of each run, Pallas kernels for 0% -> 22%
where the time goes in v1:
time: 672 us; the launch traced here: 664 us
  waiting for transfers between devices  170 us (25%)
  Pallas kernels  156 us (23%)
  local copies, waits for them, and re-layouts  130 us (19%)
  matrix products  102 us (15%)
  other arithmetic  45.9 us (7%)
  starting transfers between devices  42.2 us (6%)
  between operations  18.4 us (3%)
    ppermute x45, waiting for transfers between devices, swap(): return lax.ppermute(x, axis, [(i, i ^ mask) for i in range(size)])  170 us
    pallas_call x1, Pallas kernels, attend_backward(): pl.pallas_call(backward_kernel, grid_spec=pltpu.PrefetchScalarGridSpec(nu...  80.6 us
    pallas_call x1, Pallas kernels, attend_forward(): pl.pallas_call(forward_kernel, grid_spec=pltpu.PrefetchScalarGridSpec(num...  47.5 us
    ppermute x45, starting transfers between devices, swap(): return lax.ppermute(x, axis, [(i, i ^ mask) for i in range(size)])  42.2 us
    dot_general x4, matrix products, product(): return jnp.dot(left, right, preferred_element_type=f32)  41 us
    dot_general x8, matrix products, tail_dot(): return lax.dot_general(left, right, NT, preferred_element_type=f32)  36.6 us
    unnamed x148, local copies, waits for them, and re-layouts  31 us
    dynamic_update_slice x12, local copies, waits for them, and re-layouts, ordered(): out = lax.dynamic_update_slice_in_dim(out, piece, (s ^ k) * size, axis)  25.1 us
  transfers between devices with their start and end apart: 45, of which 20 were waited for; matrix products, arithmetic and copies ran while one was open for 22% of the time, Pallas kernels for 22%

profile of v1, /device:TPU:0, one launch (start us, length us, event | category | flops | bytes accessed | tf_op | source)
XLA Modules:
  0.0 663.7 jit_solution(13667555197346005057)
XLA Ops:
  10.4 17.0 %collective-permute-done.9 = bf16[1,496,384]{2,1,0:T(8,128)(2,1)S(1)} collective-permute-done((bf16[1,496,384]{2,1,0:T(8,128)(2,1)S(1)}, bf16[1,496,384]{2,1,0:T(8,128)(2,1)S(1)}, u32[]{:S(2)}, u32[]{:S(2)}) %collective-permute-start.9) | collective-permute-done | bytes 380960 | tf_op jit(solution)/shard_map/ppermute | solution.py:263
  31.9 20.3 %collective-permute-done.10 = bf16[2,496,384]{2,1,0:T(8,128)(2,1)S(1)} collective-permute-done((bf16[2,496,384]{2,1,0:T(8,128)(2,1)S(1)}, bf16[2,496,384]{2,1,0:T(8,128)(2,1)S(1)}, u32[]{:S(2)}, u32[]{:S(2)}) %collective-permute-start.10) | collective-permute-done | bytes 761888 | tf_op jit(solution)/shard_map/ppermute | solution.py:263
  62.5 10.3 %collective-permute-done.14 = bf16[2,384,384]{2,1,0:T(8,128)(2,1)S(1)} collective-permute-done((bf16[2,384,384]{2,1,0:T(8,128)(2,1)}, bf16[2,384,384]{2,1,0:T(8,128)(2,1)S(1)}, u32[]{:S(2)}, u32[]{:S(2)}) %collective-permute-start.14) | collective-permute-done | bytes 589856 | tf_op jit(solution)/shard_map/ppermute | solution.py:263
  78.8 11.3 %collective-permute-done.11 = bf16[4,496,384]{2,1,0:T(8,128)(2,1)} collective-permute-done((bf16[4,496,384]{2,1,0:T(8,128)(2,1)}, bf16[4,496,384]{2,1,0:T(8,128)(2,1)}, u32[]{:S(2)}, u32[]{:S(2)}) %collective-permute-start.11) | collective-permute-done | bytes 1523744 | tf_op jit(solution)/shard_map/ppermute | solution.py:263
  96.2 19.1 %collective-permute-done.15 = bf16[4,384,384]{2,1,0:T(8,128)(2,1)} collective-permute-done((bf16[4,384,384]{2,1,0:T(8,128)(2,1)}, bf16[4,384,384]{2,1,0:T(8,128)(2,1)}, u32[]{:S(2)}, u32[]{:S(2)}) %collective-permute-start.15) | collective-permute-done | bytes 1179680 | tf_op jit(solution)/shard_map/ppermute | solution.py:263
  160.0 11.5 %project.1 = (bf16[3072,256]{1,0:T(8,128)(2,1)}, bf16[3072,256]{1,0:T(8,128)(2,1)}, bf16[3072,256]{1,0:T(8,128)(2,1)}) custom-call(bf16[3072,768]{1,0:T(8,128)(2,1)} %constant_dynamic-update-slice_fusion.9.x_ref, bf16[768,768]{1,0:T(8,128)(2,1)} %fusion.31.w_ref, f32[1,768]{1,0:T(1,128)} %reshape.495.b_ref, s32[3072,1]{1,0:T(8,128)} %copy.186.doc_ref), custom_call_target="tpu_custom_call" | custom-call | tf_op jit(solution)/shard_map/project/pallas_call | solution.py:183
  171.4 47.5 %attend_forward.1 = (bf16[3072,192]{1,0:T(8,128)(2,1)}, bf16[3,3072,256]{2,1,0:T(8,128)(2,1)}) custom-call(s32[12]{0:T(128)} %get-tuple-element.230.lo_ref, s32[12]{0:T(128)} %get-tuple-element.229.hi_ref, bf16[3072,256]{1,0:T(8,128)(2,1)} %get-tuple-element.23.q_ref, bf16[3072,256]{1,0:T(8,128)(2,1)} %get-tuple-element.24.k_ref, ...), custom_call_target="tpu_custom_call" | custom-call | tf_op jit(solution)/shard_map/attend_forward/pallas_call | solution.py:192
  250.8 7.5 %join_halves.3 = bf16[8,384,768]{2,1,0:T(8,128)(2,1)} custom-call(s32[8]{0:T(128)} %gather_fusion, s32[1]{0:T(128)} %bitcast.25.c_ref, bf16[8,384,384]{2,1,0:T(8,128)(2,1)} %pad_maximum_fusion.2.own_ref, bf16[8,384,384]{2,1,0:T(8,128)(2,1)} %collective-permute-done.16.other_ref), custom_call_target="tpu_custom_call" | custom-call | tf_op jit(solution)/shard_map/join_halves/pallas_call | solution.py:320
  258.3 8.4 %join_halves.2 = bf16[8,496,768]{2,1,0:T(8,128)(2,1)} custom-call(s32[8]{0:T(128)} %gather_fusion, s32[1]{0:T(128)} %bitcast.25.c_ref, bf16[8,496,384]{2,1,0:T(8,128)(2,1)} %copy-done.4, bf16[8,496,384]{2,1,0:T(8,128)(2,1)} %collective-permute-done.12.other_ref), custom_call_target="tpu_custom_call" | custom-call | tf_op jit(solution)/shard_map/join_halves/pallas_call | solution.py:320
  276.8 31.3 %multiply_convert_fusion = (bf16[768,3072]{1,0:T(8,128)(2,1)}, f32[768,3072]{1,0:T(8,128)}, f32[768,3072]{1,0:T(8,128)}) fusion(f32[3072]{0:T(1024)S(1)} %reshape.546, bf16[768,768]{1,0:T(8,128)(2,1)S(1)} %bitcast.251, bf16[768,768]{1,0:T(8,128)(2,1)} %bitcast.253, bf16[768,768]{1,0:T(8,128)(2,1)} %bitcast.255, bf16[768,768]{1,0:T(8,128)(2,1)S(1)} %bitcast.249, ...), kind=kOutput, calls=%fused_computation.5 | convolution fusion | flops 3801415680 | bytes 30695424 | tf_op jit(solution)/shard_map/dot_general | solution.py:251
  308.1 6.1 fusion.72
  319.7 5.7 convolution_convert_fusion
  325.4 12.6 %fusion.61 = (bf16[3072]{0:T(1024)(128)(2,1)S(1)}, bf16[768,3072]{1,0:T(8,128)(2,1)}) fusion(f32[768,3072]{1,0:T(8,128)} %get-tuple-element.163, f32[768,3072]{1,0:T(8,128)} %get-tuple-element.223, f32[3072]{0:T(1024)S(1)} %reshape.546, bf16[768,768]{1,0:T(8,128)(2,1)S(1)} %get-tuple-element.155, bf16[3072,768]{1,0:T(8,128)(2,1)S(1)} %bitcast.237), kind=kOutput, calls=%fused_computation.252 | convolution fusion | flops 3661624320 | bytes 29509632 | tf_op jit(solution)/shard_map/dot_general | solution.py:259
  338.1 8.3 %multiply_reduce_fusion.1 = (bf16[768]{0:T(1024)(128)(2,1)S(1)}, f32[768]{0:T(1024)S(1)}, bf16[768]{0:T(1024)(128)(2,1)S(1)}, f32[768,768]{1,0:T(8,128)}) fusion(f32[768,768]{1,0:T(8,128)S(1)} %get-tuple-element.222, f32[768]{0:T(1024)S(1)} %fusion.47, f32[768]{0:T(1024)S(1)} %broadcast_multiply_fusion.1, f32[768]{0:T(1024)S(1)} %reshape.544, ...), kind=kOutput, calls=%fused_computation.39 | convolution fusion | flops 3648648960 | bytes 16533504 | tf_op jit(solution)/shard_map/dot_general | solution.py:259
  346.4 6.5 convolution_convert_fusion.1
  398.8 6.8 %collective-permute-done.19 = bf16[768,192]{1,0:T(8,128)(2,1)S(1)} collective-permute-done((bf16[768,192]{1,0:T(8,128)(2,1)}, bf16[768,192]{1,0:T(8,128)(2,1)S(1)}, u32[]{:S(2)}, u32[]{:S(2)}) %collective-permute-start.19) | collective-permute-done | bytes 294944 | tf_op jit(solution)/shard_map/ppermute | solution.py:263
  406.8 80.6 %attend_backward.1 = (bf16[3072,256]{1,0:T(8,128)(2,1)}, bf16[3072,512]{1,0:T(8,128)(2,1)}) custom-call(s32[12]{0:T(128)} %get-tuple-element.230.lo_ref, s32[12]{0:T(128)} %get-tuple-element.229.hi_ref, bf16[3,3072,256]{2,1,0:T(8,128)(2,1)} %get-tuple-element.27.qa_ref, bf16[3072,256]{1,0:T(8,128)(2,1)} %get-tuple-element.24.k_ref, ...), custom_call_target="tpu_custom_call" | custom-call | tf_op jit(solution)/shard_map/attend_backward/pallas_call | solution.py:206
  490.0 7.9 %convolution_convert_fusion.4 = bf16[768,768]{1,0:T(8,128)(2,1)S(1)} fusion(bf16[3072,768]{1,0:T(8,128)(2,1)} %constant_dynamic-update-slice_fusion.9.x_ref, bf16[3072,768]{1,0:T(8,128)(2,1)S(1)} %constant_dynamic-update-slice_fusion.2), kind=kOutput, calls=%fused_computation.54 | convolution fusion | flops 3624468480 | bytes 10616832 | tf_op jit(solution)/shard_map/dot_general | solution.py:255
  503.4 5.7 convolution_convert_fusion.2
  518.7 6.8 %collective-permute-done.28 = bf16[4,114,384]{2,1,0:T(8,128)(2,1)S(1)} collective-permute-done((bf16[4,114,384]{2,1,0:T(8,128)(2,1)S(1)}, bf16[4,114,384]{2,1,0:T(8,128)(2,1)S(1)}, u32[]{:S(2)}, u32[]{:S(2)}) %collective-permute-start.28) | collective-permute-done | bytes 350240 | tf_op jit(solution)/shard_map/ppermute | solution.py:263
  534.7 6.6 collective-permute-done.30
  594.0 18.7 %collective-permute-done.40 = bf16[4,384,384]{2,1,0:T(8,128)(2,1)S(1)} collective-permute-done((bf16[4,384,384]{2,1,0:T(8,128)(2,1)S(1)}, bf16[4,384,384]{2,1,0:T(8,128)(2,1)S(1)}, u32[]{:S(2)}, u32[]{:S(2)}) %collective-permute-start.40) | collective-permute-done | bytes 1179680 | tf_op jit(solution)/shard_map/ppermute | solution.py:263
  615.5 18.8 %collective-permute-done.41 = bf16[2,384,384]{2,1,0:T(8,128)(2,1)S(1)} collective-permute-done((bf16[2,384,384]{2,1,0:T(8,128)(2,1)S(1)}, bf16[2,384,384]{2,1,0:T(8,128)(2,1)S(1)}, u32[]{:S(2)}, u32[]{:S(2)}) %collective-permute-start.41) | collective-permute-done | bytes 589856 | tf_op jit(solution)/shard_map/ppermute | solution.py:263
  640.4 9.8 %collective-permute-done.42 = bf16[1,384,384]{2,1,0:T(8,128)(2,1)} collective-permute-done((bf16[1,384,384]{2,1,0:T(8,128)(2,1)}, bf16[1,384,384]{2,1,0:T(8,128)(2,1)}, u32[]{:S(2)}, u32[]{:S(2)}) %collective-permute-start.42) | collective-permute-done | bytes 294944 | tf_op jit(solution)/shard_map/ppermute | solution.py:263
  (445 shorter events, 260.2 us)
Async XLA Ops:
  6.2 21.1 %collective-permute-start.9 = (bf16[1,496,384]{2,1,0:T(8,128)(2,1)S(1)}, bf16[1,496,384]{2,1,0:T(8,128)(2,1)S(1)}, u32[]{:S(2)}, u32[]{:S(2)}) collective-permute-start(bf16[1,496,384]{2,1,0:T(8,128)(2,1)S(1)} %dynamic-slice_bitcast_fusion.6), channel_id=1, source_target_pairs={{0,16},{4,20},{8,24},{12,28},{16,0},{20,4},{24,8},{28,12},{1,17},{... | collective-permute-start | bytes 1142792 | tf_op jit(solution)/shard_map/ppermute | solution.py:263
  27.6 24.6 %collective-permute-start.10 = (bf16[2,496,384]{2,1,0:T(8,128)(2,1)S(1)}, bf16[2,496,384]{2,1,0:T(8,128)(2,1)S(1)}, u32[]{:S(2)}, u32[]{:S(2)}) collective-permute-start(bf16[2,496,384]{2,1,0:T(8,128)(2,1)S(1)} %pad_maximum_fusion.9), channel_id=1, source_target_pairs={{0,8},{4,12},{8,0},{12,4},{16,24},{20,28},{24,16},{28,20},{1,9},{5... | collective-permute-start | bytes 2285576 | tf_op jit(solution)/shard_map/ppermute | solution.py:263
  28.4 26.4 %collective-permute-start.13 = (bf16[1,384,384]{2,1,0:T(8,128)(2,1)S(1)}, bf16[1,384,384]{2,1,0:T(8,128)(2,1)S(1)}, u32[]{:S(2)}, u32[]{:S(2)}) collective-permute-start(bf16[1,384,384]{2,1,0:T(8,128)(2,1)S(1)} %dynamic-slice_bitcast_fusion.9), channel_id=1, source_target_pairs={{0,16},{4,20},{8,24},{12,28},{16,0},{20,4},{24,8},{28,12},{1,17},{... | collective-permute-start | bytes 884744 | tf_op jit(solution)/shard_map/ppermute | solution.py:263
  53.5 36.5 %collective-permute-start.11 = (bf16[4,496,384]{2,1,0:T(8,128)(2,1)}, bf16[4,496,384]{2,1,0:T(8,128)(2,1)}, u32[]{:S(2)}, u32[]{:S(2)}) collective-permute-start(bf16[4,496,384]{2,1,0:T(8,128)(2,1)} %pad_maximum_fusion.3), channel_id=1, source_target_pairs={{0,4},{4,0},{8,12},{12,8},{16,20},{20,16},{24,28},{28,24},{1,5},{5... | collective-permute-start | bytes 4571144 | tf_op jit(solution)/shard_map/ppermute | solution.py:263
  57.8 19.6 %collective-permute-start.3 = (bf16[1,98,768]{2,1,0:T(8,128)(2,1)S(1)}, bf16[1,98,768]{2,1,0:T(8,128)(2,1)S(1)}, u32[]{:S(2)}, u32[]{:S(2)}) collective-permute-start(bf16[1,98,768]{2,1,0:T(8,128)(2,1)S(1)} %maximum_bitcast_fusion), channel_id=1, source_target_pairs={{0,16},{4,20},{8,24},{12,28},{16,0},{20,4},{24,8},{28,12},{1,17},{... | collective-permute-start | bytes 451592 | tf_op jit(solution)/shard_map/ppermute | solution.py:263
  74.0 41.4 %collective-permute-start.15 = (bf16[4,384,384]{2,1,0:T(8,128)(2,1)}, bf16[4,384,384]{2,1,0:T(8,128)(2,1)}, u32[]{:S(2)}, u32[]{:S(2)}) collective-permute-start(bf16[4,384,384]{2,1,0:T(8,128)(2,1)} %pad_maximum_fusion.6), channel_id=1, source_target_pairs={{0,4},{4,0},{8,12},{12,8},{16,20},{20,16},{24,28},{28,24},{1,5},{5... | collective-permute-start | bytes 3538952 | tf_op jit(solution)/shard_map/ppermute | solution.py:263
  75.4 65.8 %collective-permute-start.1 = (bf16[768,768]{1,0:T(8,128)(2,1)}, bf16[768,768]{1,0:T(8,128)(2,1)}, u32[]{:S(2)}, u32[]{:S(2)}) collective-permute-start(bf16[768,768]{1,0:T(8,128)(2,1)} %bitcast.257), channel_id=1, source_target_pairs={{0,2},{1,3},{2,0},{3,1},{4,6},{5,7},{6,4},{7,5},{8,10},{9,11},{10,... | collective-permute-start | bytes 3538952 | tf_op jit(solution)/shard_map/ppermute | solution.py:263
  77.0 77.1 %collective-permute-start = (bf16[768,768]{1,0:T(8,128)(2,1)}, bf16[768,768]{1,0:T(8,128)(2,1)}, u32[]{:S(2)}, u32[]{:S(2)}) collective-permute-start(bf16[768,768]{1,0:T(8,128)(2,1)} %bitcast.258), channel_id=1, source_target_pairs={{0,1},{1,0},{2,3},{3,2},{4,5},{5,4},{6,7},{7,6},{8,9},{9,8},{10,11... | collective-permute-start | bytes 3538952 | tf_op jit(solution)/shard_map/ppermute | solution.py:263
  92.0 166.3 %collective-permute-start.12 = (bf16[8,496,384]{2,1,0:T(8,128)(2,1)S(1)}, bf16[8,496,384]{2,1,0:T(8,128)(2,1)}, u32[]{:S(2)}, u32[]{:S(2)}) collective-permute-start(bf16[8,496,384]{2,1,0:T(8,128)(2,1)S(1)} %pad_maximum_fusion.1.own_ref), channel_id=1, source_target_pairs={{0,1},{1,0},{2,3},{3,2},{4,5},{5,4},{6,7},{7,6},{8,9},{9,8},{10,11... | collective-permute-start | bytes 9142280 | tf_op jit(solution)/shard_map/ppermute | solution.py:263
  94.5 42.0 %collective-permute-start.5 = (bf16[4,98,768]{2,0,1:T(4,128)(2,1)}, bf16[4,98,768]{2,0,1:T(4,128)(2,1)}, u32[]{:S(2)}, u32[]{:S(2)}) collective-permute-start(bf16[4,98,768]{2,0,1:T(4,128)(2,1)} %copy.184), channel_id=1, source_target_pairs={{0,4},{4,0},{8,12},{12,8},{16,20},{20,16},{24,28},{28,24},{1,5},{5... | collective-permute-start | bytes 1806344 | tf_op jit(solution)/shard_map/ppermute | solution.py:263
  118.3 132.5 %collective-permute-start.16 = (bf16[8,384,384]{2,1,0:T(8,128)(2,1)}, bf16[8,384,384]{2,1,0:T(8,128)(2,1)}, u32[]{:S(2)}, u32[]{:S(2)}) collective-permute-start(bf16[8,384,384]{2,1,0:T(8,128)(2,1)} %pad_maximum_fusion.2.own_ref), channel_id=1, source_target_pairs={{0,1},{1,0},{2,3},{3,2},{4,5},{5,4},{6,7},{7,6},{8,9},{9,8},{10,11... | collective-permute-start | bytes 7077896 | tf_op jit(solution)/shard_map/ppermute | solution.py:263
  221.5 24.7 %collective-permute-start.8 = (bf16[768,192]{1,0:T(8,128)(2,1)}, bf16[768,192]{1,0:T(8,128)(2,1)}, u32[]{:S(2)}, u32[]{:S(2)}) collective-permute-start(bf16[768,192]{1,0:T(8,128)(2,1)} %get-tuple-element.169), channel_id=1, source_target_pairs={{0,3},{1,2},{2,1},{3,0},{4,7},{5,6},{6,5},{7,4},{8,11},{9,10},{10,... | collective-permute-start | bytes 884744 | tf_op jit(solution)/shard_map/ppermute | solution.py:263
  222.7 18.9 %collective-permute-start.7 = (bf16[768,192]{1,0:T(8,128)(2,1)}, bf16[768,192]{1,0:T(8,128)(2,1)}, u32[]{:S(2)}, u32[]{:S(2)}) collective-permute-start(bf16[768,192]{1,0:T(8,128)(2,1)} %get-tuple-element.170), channel_id=1, source_target_pairs={{0,2},{1,3},{2,0},{3,1},{4,6},{5,7},{6,4},{7,5},{8,10},{9,11},{10,... | collective-permute-start | bytes 884744 | tf_op jit(solution)/shard_map/ppermute | solution.py:263
  387.4 18.2 %collective-permute-start.19 = (bf16[768,192]{1,0:T(8,128)(2,1)}, bf16[768,192]{1,0:T(8,128)(2,1)S(1)}, u32[]{:S(2)}, u32[]{:S(2)}) collective-permute-start(bf16[768,192]{1,0:T(8,128)(2,1)} %copy.193), channel_id=1, source_target_pairs={{0,3},{1,2},{2,1},{3,0},{4,7},{5,6},{6,5},{7,4},{8,11},{9,10},{10,... | collective-permute-start | bytes 884744 | tf_op jit(solution)/shard_map/ppermute | solution.py:263
  391.2 120.9 %collective-permute-start.27 = (bf16[8,114,384]{2,0,1:T(8,128)(2,1)}, bf16[8,114,384]{2,0,1:T(8,128)(2,1)}, u32[]{:S(2)}, u32[]{:S(2)}) collective-permute-start(bf16[8,114,384]{2,0,1:T(8,128)(2,1)} %copy.207), channel_id=1, source_target_pairs={{0,1},{1,0},{2,3},{3,2},{4,5},{5,4},{6,7},{7,6},{8,9},{9,8},{10,11... | collective-permute-start | bytes 2101256 | tf_op jit(solution)/shard_map/ppermute | solution.py:263
  398.0 156.2 %collective-permute-start.33 = (bf16[8,96,1536]{2,1,0:T(8,128)(2,1)}, bf16[8,96,1536]{2,1,0:T(8,128)(2,1)}, u32[]{:S(2)}, u32[]{:S(2)}) collective-permute-start(bf16[8,96,1536]{2,1,0:T(8,128)(2,1)} %constant_dynamic-slice_fusion.7), channel_id=1, source_target_pairs={{0,1},{1,0},{2,3},{3,2},{4,5},{5,4},{6,7},{7,6},{8,9},{9,8},{10,11... | collective-permute-start | bytes 7077896 | tf_op jit(solution)/shard_map/ppermute | solution.py:263
  398.5 182.8 %collective-permute-start.39 = (bf16[8,384,384]{2,1,0:T(8,128)(2,1)}, bf16[8,384,384]{2,1,0:T(8,128)(2,1)}, u32[]{:S(2)}, u32[]{:S(2)}) collective-permute-start(bf16[8,384,384]{2,1,0:T(8,128)(2,1)} %constant_dynamic-slice_fusion.5), channel_id=1, source_target_pairs={{0,1},{1,0},{2,3},{3,2},{4,5},{5,4},{6,7},{7,6},{8,9},{9,8},{10,11... | collective-permute-start | bytes 7077896 | tf_op jit(solution)/shard_map/ppermute | solution.py:263
  512.0 76.8 %collective-permute-start.20 = (bf16[2,768,768]{2,1,0:T(8,128)(2,1)}, bf16[2,768,768]{2,1,0:T(8,128)(2,1)}, u32[]{:S(2)}, u32[]{:S(2)}) collective-permute-start(bf16[2,768,768]{2,1,0:T(8,128)(2,1)} %dynamic-slice_bitcast_fusion), channel_id=1, source_target_pairs={{0,1},{1,0},{2,3},{3,2},{4,5},{5,4},{6,7},{7,6},{8,9},{9,8},{10,11... | collective-permute-start | bytes 7077896 | tf_op jit(solution)/shard_map/ppermute | solution.py:263
  558.4 28.7 %collective-permute-start.34 = (bf16[4,96,1536]{2,1,0:T(8,128)(2,1)}, bf16[4,96,1536]{2,1,0:T(8,128)(2,1)}, u32[]{:S(2)}, u32[]{:S(2)}) collective-permute-start(bf16[4,96,1536]{2,1,0:T(8,128)(2,1)} %dynamic-slice_bitcast_fusion.2), channel_id=1, source_target_pairs={{0,4},{4,0},{8,12},{12,8},{16,20},{20,16},{24,28},{28,24},{1,5},{5... | collective-permute-start | bytes 3538952 | tf_op jit(solution)/shard_map/ppermute | solution.py:263
  584.5 28.2 %collective-permute-start.40 = (bf16[4,384,384]{2,1,0:T(8,128)(2,1)S(1)}, bf16[4,384,384]{2,1,0:T(8,128)(2,1)S(1)}, u32[]{:S(2)}, u32[]{:S(2)}) collective-permute-start(bf16[4,384,384]{2,1,0:T(8,128)(2,1)S(1)} %dynamic-slice_bitcast_fusion.1), channel_id=1, source_target_pairs={{0,4},{4,0},{8,12},{12,8},{16,20},{20,16},{24,28},{28,24},{1,5},{5... | collective-permute-start | bytes 3538952 | tf_op jit(solution)/shard_map/ppermute | solution.py:263
  588.7 24.4 %collective-permute-start.35 = (bf16[2,96,1536]{2,1,0:T(8,128)(2,1)S(1)}, bf16[2,96,1536]{2,1,0:T(8,128)(2,1)S(1)}, u32[]{:S(2)}, u32[]{:S(2)}) collective-permute-start(bf16[2,96,1536]{2,1,0:T(8,128)(2,1)S(1)} %dynamic-slice_bitcast_fusion.5), channel_id=1, source_target_pairs={{0,8},{4,12},{8,0},{12,4},{16,24},{20,28},{24,16},{28,20},{1,9},{5... | collective-permute-start | bytes 1769480 | tf_op jit(solution)/shard_map/ppermute | solution.py:263
  592.3 62.2 %collective-permute-start.21 = (bf16[768,768]{1,0:T(8,128)(2,1)}, bf16[768,768]{1,0:T(8,128)(2,1)}, u32[]{:S(2)}, u32[]{:S(2)}) collective-permute-start(bf16[768,768]{1,0:T(8,128)(2,1)} %dynamic-slice_bitcast_fusion.3), channel_id=1, source_target_pairs={{0,2},{1,3},{2,0},{3,1},{4,6},{5,7},{6,4},{7,5},{8,10},{9,11},{10,... | collective-permute-start | bytes 3538952 | tf_op jit(solution)/shard_map/ppermute | solution.py:263
  613.1 21.1 %collective-permute-start.41 = (bf16[2,384,384]{2,1,0:T(8,128)(2,1)S(1)}, bf16[2,384,384]{2,1,0:T(8,128)(2,1)S(1)}, u32[]{:S(2)}, u32[]{:S(2)}) collective-permute-start(bf16[2,384,384]{2,1,0:T(8,128)(2,1)S(1)} %dynamic-slice_bitcast_fusion.4), channel_id=1, source_target_pairs={{0,8},{4,12},{8,0},{12,4},{16,24},{20,28},{24,16},{28,20},{1,9},{5... | collective-permute-start | bytes 1769480 | tf_op jit(solution)/shard_map/ppermute | solution.py:263
  613.4 22.6 %collective-permute-start.36 = (bf16[1,96,1536]{2,1,0:T(8,128)(2,1)S(1)}, bf16[1,96,1536]{2,1,0:T(8,128)(2,1)S(1)}, u32[]{:S(2)}, u32[]{:S(2)}) collective-permute-start(bf16[1,96,1536]{2,1,0:T(8,128)(2,1)S(1)} %constant_dynamic-slice_fusion.6), channel_id=1, source_target_pairs={{0,16},{4,20},{8,24},{12,28},{16,0},{20,4},{24,8},{28,12},{1,17},{... | collective-permute-start | bytes 884744 | tf_op jit(solution)/shard_map/ppermute | solution.py:263
  (87 other events, 1159.3 us)

commit v2 on v1

v2 whole, which is shorter than its diff:
```python
import jax
import jax.numpy as jnp
from functools import partial
from jax import lax
from jax.experimental import pallas as pl
from jax.experimental.pallas import tpu as pltpu
from jax.sharding import PartitionSpec as P

D = 768
H = 12
HD = 64
FF = 3072
EMB = 128
HEADS = 3
OWN = HEADS * HD
NORM_EPS = 1e-12
UNIT_EPS = 1e-06
BLK = 256
LANES = 256
DOC_LANE = 192
STAT_LANE = 200
FAR = 2.0 ** 30
NT = (((1,), (1,)), ((), ()))
TN = (((0,), (0,)), ((), ()))
f32, bf16 = jnp.float32, jnp.bfloat16
VM = 62 * 1024 * 1024


def lane_of(shape):
    return lax.broadcasted_iota(jnp.int32, shape, 1)


def three_terms(x, lane):
    top = x.astype(bf16).astype(f32)
    mid = (x - top).astype(bf16).astype(f32)
    rest = x - top - mid
    return jnp.where(lane == STAT_LANE, top, jnp.where(lane == STAT_LANE + 1, mid, rest))


def is_stat(lane):
    return (lane >= STAT_LANE) & (lane < STAT_LANE + 3)


def own_lanes(lane, h):
    return (lane >= h * HD) & (lane < h * HD + HD)


def params(**more):
    return pltpu.CompilerParams(dimension_semantics=("arbitrary",), vmem_limit_bytes=VM, **more)


def whole(shape):
    return pl.BlockSpec(shape, lambda *_: (0,) * len(shape))


def cost(flops, moved):
    return pl.CostEstimate(flops=int(flops), bytes_accessed=int(moved), transcendentals=0)


def masks(size):
    out = []
    m = 1
    while m < size:
        out.append(m)
        m *= 2
    return out


def full_order(n):
    half = held_order(n)
    return half + [k ^ 1 for k in half]


def held_order(n):
    seen = [0]
    for m in reversed(masks(n)[1:]):
        seen = seen + [k ^ m for k in seen]
    return seen


def project_kernel(n, pieces, full, at_ref, *refs):
    xs, refs = refs[:pieces], refs[pieces:]
    if full:
        w_in, b_ref, doc_ref, refs = refs[0], refs[1], refs[2], refs[3:]
    else:
        lo_ref, hi_ref, b_ref, doc_ref, refs = refs[0], refs[1], refs[2], refs[3], refs[4:]
    q_ref, k_ref, v_ref, w = refs[-4:]
    step = pl.program_id(0)
    own = D // n

    @pl.when(step == 0)
    def _():
        zero = jnp.zeros((D, LANES - OWN), bf16)
        for j in range(3):
            w[:, j * LANES + OWN:(j + 1) * LANES] = zero
        if full:
            for j in range(3):
                w[:, j * LANES:j * LANES + OWN] = w_in[:, j * OWN:(j + 1) * OWN]
        else:
            for ref, extra in ((lo_ref, 0), (hi_ref, 1)):
                for p, diff in enumerate(held_order(n)):
                    rows = pl.ds(pl.multiple_of((at_ref[1] ^ (diff ^ extra)) * own, 16), own)
                    for j in range(3):
                        w[rows, j * LANES:j * LANES + OWN] = ref[p, :own, j * OWN:(j + 1) * OWN]

    def body(x_ref):
        x = x_ref[...]
        lane = lane_of((x.shape[0], LANES))
        hot = lane - DOC_LANE == doc_ref[...]
        docs = (lane >= DOC_LANE) & (lane < STAT_LANE)

        def part(j):
            y = jnp.dot(x, w[:, j * LANES:(j + 1) * LANES], preferred_element_type=f32)
            return (y + b_ref[:, j * LANES:(j + 1) * LANES]).astype(bf16)
        q = part(0).astype(f32) * (HD ** -0.5)
        q_ref[...] = jnp.where(hot, -FAR, q).astype(bf16)
        k_ref[...] = jnp.where(docs & ~hot | is_stat(lane), 1.0, part(1).astype(f32)).astype(bf16)
        v_ref[...] = jnp.where(is_stat(lane), 1.0, part(2).astype(f32)).astype(bf16)
    for p in range(pieces):
        pl.when(step == p)(partial(body, xs[p]))


def project(n, at, xs, diffs, weights, bias, doc, into=None):
    rows = xs[0].shape[0]
    full = len(weights) == 1

    def place(t, at):
        diff = diffs[0]
        for p in range(1, len(diffs)):
            diff = jnp.where(t == p, diffs[p], diff)
        return (at[0] ^ diff, 0)
    spec = pl.BlockSpec((rows, LANES), place)
    any_spec = pl.BlockSpec(memory_space=pl.ANY)
    ins = [whole(x.shape) for x in xs] + [whole(w.shape) for w in weights] + [whole(bias.shape), pl.BlockSpec((rows, 1), place)]
    args = list(xs) + list(weights) + [bias, doc]
    alias = {}
    if into is not None:
        alias = {1 + len(args) + j: j for j in range(3)}
        args += list(into)
        ins += [any_spec] * 3
    shape = jax.ShapeDtypeStruct((4 * rows, LANES), bf16)
    return pl.pallas_call(
        partial(project_kernel, n, len(xs), full),
        grid_spec=pltpu.PrefetchScalarGridSpec(
            num_scalar_prefetch=1, grid=(len(xs),), in_specs=ins, out_specs=[spec] * 3,
            scratch_shapes=[pltpu.VMEM((D, 3 * LANES), bf16)]),
        out_shape=[shape] * 3, input_output_aliases=alias, compiler_params=params(),
        cost_estimate=cost(len(xs) * rows * D * 3 * LANES * 4, 8e6), name="project")(at, *args)


def forward_kernel(at_ref, lo_ref, hi_ref, q_ref, k_ref, v_ref, *refs):
    ctx_ref, qa_ref, vm, scr, acc, qm, peak = refs[-7:]
    steps = pl.num_programs(0)
    first = at_ref[0] * steps
    qb = first + pl.program_id(0)
    lane = lane_of((BLK, LANES))

    @pl.when(pl.program_id(0) == 0)
    def _():
        def fill(t, _):
            rows = pl.ds(pl.multiple_of(t * BLK, BLK), BLK)
            v = v_ref[rows, :].astype(f32)
            for h in range(HEADS):
                vm[h, rows, :] = jnp.where(own_lanes(lane, h), v, jnp.where(lane == DOC_LANE + h, 1.0, 0.0)).astype(bf16)
            return 0
        lax.fori_loop(lo_ref[first], hi_ref[first + steps - 1], fill, 0)

    lo, hi = lo_ref[qb], hi_ref[qb]
    q = q_ref[...].astype(f32)
    acc[...] = jnp.zeros_like(acc)
    masked = [jnp.where(own_lanes(lane, h) | (lane >= DOC_LANE), q, 0.0) for h in range(HEADS)]
    for h in range(HEADS):
        qm[h] = masked[h].astype(bf16)
        peak[h] = jnp.full((BLK, 128), -jnp.inf, f32)

    def score(kb, _):
        keys = k_ref[pl.ds(pl.multiple_of(kb * BLK, BLK), BLK), :]
        for h in range(HEADS):
            s = lax.dot_general(qm[h], keys, NT, preferred_element_type=f32)
            scr[h, kb - lo] = s
            peak[h] = jnp.maximum(peak[h], jnp.maximum(s[:, :128], s[:, 128:]))
        return 0
    lax.fori_loop(lo, hi, score, 0)
    tops = [jnp.max(peak[h], axis=1, keepdims=True) for h in range(HEADS)]
    for h in range(HEADS):
        peak[h] = jnp.broadcast_to(tops[h], (BLK, 128))

    def mix(kb, _):
        parts = []
        for h in range(HEADS):
            top = peak[h]
            s = scr[h, kb - lo]
            p = jnp.exp(s - jnp.concatenate([top, top], axis=1)).astype(bf16)
            parts.append(jnp.dot(p, vm[h, pl.ds(pl.multiple_of(kb * BLK, BLK), BLK), :], preferred_element_type=f32))
        acc[...] += parts[0] + parts[1] + parts[2]
        return 0
    lax.fori_loop(lo, hi, mix, 0)
    out = acc[...]
    totals = [out[:, DOC_LANE + h:DOC_LANE + h + 1] for h in range(HEADS)]
    inv = jnp.where(lane < HD, 1.0 / totals[0], jnp.where(lane < 2 * HD, 1.0 / totals[1], 1.0 / totals[2]))
    ctx_ref[...] = (out * inv).astype(bf16)[:, :OWN]
    for h in range(HEADS):
        lse = tops[h] + jnp.log(totals[h])
        qa_ref[h] = jnp.where(is_stat(lane), three_terms(-lse + jnp.zeros((BLK, LANES), f32), lane), masked[h]).astype(bf16)


def attend_forward(block, lo, hi, q, k, v, into=None):
    length = q.shape[0]
    rows = length // 4
    steps = rows // BLK
    args, alias = [q, k, v], {}
    ins = [pl.BlockSpec((BLK, LANES), lambda i, at, *_: (at[0] * steps + i, 0)), whole((length, LANES)), whole((length, LANES))]
    if into is not None:
        alias = {3 + len(args): 1}
        args.append(into)
        ins.append(pl.BlockSpec(memory_space=pl.ANY))
    return pl.pallas_call(
        forward_kernel,
        grid_spec=pltpu.PrefetchScalarGridSpec(
            num_scalar_prefetch=3, grid=(steps,), in_specs=ins,
            out_specs=[pl.BlockSpec((BLK, OWN), lambda i, *_: (i, 0)), pl.BlockSpec((HEADS, BLK, LANES), lambda i, at, *_: (0, at[0] * steps + i, 0))],
            scratch_shapes=[pltpu.VMEM((HEADS, length, LANES), bf16), pltpu.VMEM((HEADS, length // BLK, BLK, BLK), f32), pltpu.VMEM((BLK, LANES), f32),
                            pltpu.VMEM((HEADS, BLK, LANES), bf16), pltpu.VMEM((HEADS, BLK, 128), f32)]),
        out_shape=[jax.ShapeDtypeStruct((rows, OWN), bf16), jax.ShapeDtypeStruct((HEADS, length, LANES), bf16)],
        input_output_aliases=alias, compiler_params=params(), cost_estimate=cost(8e9, 8e6), name="attend_forward")(block, lo, hi, *args)


def backward_kernel(at_ref, lo_ref, hi_ref, qa_ref, k_ref, v_ref, *refs):
    os, dos = refs[:4], refs[4:8]
    dqkv_ref, km, dm, dqs, dks, dvs = refs[8:]
    kb = pl.program_id(0)
    length = k_ref.shape[0]
    rows4 = length // 4
    lane = lane_of((BLK, LANES))

    @pl.when(kb == 0)
    def _():
        row = lax.broadcasted_iota(jnp.int32, (OWN, LANES), 0)
        col = lane_of((OWN, LANES))
        picks = [jnp.where((row >= h * HD) & (row < h * HD + HD) & is_stat(col), -1.0, 0.0).astype(bf16) for h in range(HEADS)]
        for d in range(4):
            def fill(t, _, d=d):
                here = pl.ds(pl.multiple_of(t * BLK, BLK), BLK)
                rows = pl.ds(pl.multiple_of((at_ref[0] ^ d) * rows4 + t * BLK, BLK), BLK)
                k = k_ref[rows, :].astype(f32)
                do = dos[d][here, :].astype(f32)
                prod = do * os[d][here, :].astype(f32)
                top = prod.astype(bf16)
                rest = (prod - top.astype(f32)).astype(bf16)
                do = jnp.concatenate([do, jnp.zeros((BLK, LANES - OWN), f32)], axis=1)
                for h in range(HEADS):
                    inner = jnp.dot(top, picks[h], preferred_element_type=f32) + jnp.dot(rest, picks[h], preferred_element_type=f32)
                    km[h, rows, :] = jnp.where(own_lanes(lane, h), k, 0.0).astype(bf16)
                    dm[h, rows, :] = jnp.where(is_stat(lane), three_terms(inner, lane), jnp.where(own_lanes(lane, h), do, 0.0)).astype(bf16)
                dqs[rows, :] = jnp.zeros((BLK, LANES), f32)
                return 0
            lax.fori_loop(0, rows4 // BLK, fill, 0)

    dks[...] = jnp.zeros_like(dks)
    dvs[...] = jnp.zeros_like(dvs)
    here = pl.ds(pl.multiple_of(kb * BLK, BLK), BLK)
    k = k_ref[here, :]
    v = v_ref[here, :]

    def pair(qb, _):
        rows = pl.ds(pl.multiple_of(qb * BLK, BLK), BLK)
        dsl, dkl, dvl = [], [], []
        for h in range(HEADS):
            qa = qa_ref[h, rows, :]
            da = dm[h, rows, :]
            p = jnp.exp(lax.dot_general(k, qa, NT, preferred_element_type=f32))
            dp = lax.dot_general(v, da, NT, preferred_element_type=f32)
            ds = (p * dp).astype(bf16)
            dvl.append(jnp.dot(p.astype(bf16), da, preferred_element_type=f32))
            dkl.append(jnp.dot(ds, qa, preferred_element_type=f32))
            dsl.append(lax.dot_general(ds, km[h, here, :], TN, preferred_element_type=f32))
        dvs[...] += dvl[0] + dvl[1] + dvl[2]
        dks[...] += dkl[0] + dkl[1] + dkl[2]
        dqs[rows, :] += dsl[0] + dsl[1] + dsl[2]
        return 0
    lax.fori_loop(lo_ref[kb], hi_ref[kb], pair, 0)
    keep = lane < OWN
    dqkv_ref[here, LANES:2 * LANES] = jnp.where(keep, dks[...], 0.0).astype(bf16)
    dqkv_ref[here, 2 * LANES:] = jnp.where(keep, dvs[...], 0.0).astype(bf16)

    @pl.when(kb == pl.num_programs(0) - 1)
    def _():
        def drain(t, _):
            rows = pl.ds(pl.multiple_of(t * BLK, BLK), BLK)
            dqkv_ref[rows, :LANES] = (dqs[rows, :] * (HD ** -0.5)).astype(bf16)
            return 0
        lax.fori_loop(0, length // BLK, drain, 0)


def attend_backward(at, lo, hi, qa, k, v, os, dos):
    length = k.shape[0]
    return pl.pallas_call(
        backward_kernel,
        grid_spec=pltpu.PrefetchScalarGridSpec(
            num_scalar_prefetch=3, grid=(length // BLK,),
            in_specs=[whole((HEADS, length, LANES)), whole((length, LANES)), whole((length, LANES))] + [whole(o.shape) for o in os] + [whole(o.shape) for o in dos],
            out_specs=whole((length, 3 * LANES)),
            scratch_shapes=[pltpu.VMEM((HEADS, length, LANES), bf16), pltpu.VMEM((HEADS, length, LANES), bf16), pltpu.VMEM((length, LANES), f32),
                            pltpu.VMEM((BLK, LANES), f32), pltpu.VMEM((BLK, LANES), f32)]),
        out_shape=jax.ShapeDtypeStruct((length, 3 * LANES), bf16),
        compiler_params=params(), cost_estimate=cost(60e9, 16e6), name="attend_backward")(at, lo, hi, qa, k, v, *os, *dos)


def block_ranges(doc_row):
    first = doc_row[::BLK]
    last = doc_row[BLK - 1::BLK]
    begin = jnp.sum((doc_row[None, :] < first[:, None]).astype(jnp.int32), axis=1)
    end = jnp.sum((doc_row[None, :] <= last[:, None]).astype(jnp.int32), axis=1)
    return begin // BLK, (end + BLK - 1) // BLK


TAIL_SCALE = 0.42 * 0.5 ** 0.5
TAIL_TERMS = (0.23682439212296424, 0.23958346194522595, 0.1947406331574046, 0.2686953149002349,
              -0.1304376234380357, 0.44057671758205813, -0.3202007968326042, 0.07021773093534588)


def gelu_and_slope(x):
    t = 1.0 / (1.0 + TAIL_SCALE * jnp.abs(x))
    bell = jnp.exp(-0.5 * x * x)
    poly = 0.5 * TAIL_TERMS[-1]
    for term in TAIL_TERMS[-2::-1]:
        poly = poly * t + 0.5 * term
    tail = poly * t * bell
    phi = jnp.where(x < 0, tail, 1.0 - tail)
    return x * phi, phi + x * bell * (0.5 / 3.141592653589793) ** 0.5


def norm(resid, gain, shift):
    center = resid - jnp.mean(resid, axis=-1, keepdims=True)
    spread = jnp.mean(center * center, axis=-1, keepdims=True)
    r = lax.rsqrt(spread + NORM_EPS)
    unit = center * r
    return unit, r, unit * gain + shift


def norm_back(d_out, unit, r, gain):
    d_n = d_out * gain
    return r * (d_n - jnp.mean(d_n, axis=-1, keepdims=True) - unit * jnp.mean(d_n * unit, axis=-1, keepdims=True))


CHUNK = 512


def dense_body(s, step, ctx, tok, cot, vec, bias_up, w_o, w_up, w_dn, w_pr, outs, slope):
    embed_ref, res1_ref, act_ref, dpre_ref, h1_ref, dffn_ref, dattn_ref, dc0, dc1, dc2, dc3, gvec, gup, gproj = outs

    @pl.when(step == 0)
    def _():
        gvec[...] = jnp.zeros_like(gvec)
        gup[...] = jnp.zeros_like(gup)
        gproj[...] = jnp.zeros_like(gproj)

    def heads_rows(d):
        return w_o[pl.ds(pl.multiple_of((s ^ d) * OWN, 64), OWN), :]
    attn = vec[0:1, :] + jnp.dot(ctx[0][...], heads_rows(0), preferred_element_type=f32)
    for d in range(1, 4):
        attn += jnp.dot(ctx[d][...], heads_rows(d), preferred_element_type=f32)
    gain1, gain2 = vec[1:2, :], vec[4:5, :]
    n1, r1, h1 = norm(tok[...].astype(f32) + attn, gain1, vec[2:3, :])
    low1 = h1.astype(bf16)
    h1_ref[...] = low1
    ffn = jnp.zeros(h1.shape, f32)
    for j in range(FF // CHUNK):
        cols = slice(j * CHUNK, (j + 1) * CHUNK)
        pre = jnp.dot(low1, w_up[:, cols], preferred_element_type=f32) + bias_up[:, cols]
        act, rise = gelu_and_slope(pre)
        slope[:, cols] = rise
        act = act.astype(bf16)
        act_ref[:, cols] = act
        ffn += jnp.dot(act, w_dn[cols, :], preferred_element_type=f32)
    n2, r2, h2 = norm(h1 + (ffn + vec[3:4, :]), gain2, vec[5:6, :])
    low2 = h2.astype(bf16)
    proj = jnp.dot(low2, w_pr[...], preferred_element_type=f32)
    inv = lax.rsqrt(jnp.sum(proj * proj, axis=-1, keepdims=True) + UNIT_EPS)
    emb = proj * inv
    embed_ref[...] = emb
    pull = cot[...].astype(f32)
    d_proj = ((pull - emb * jnp.sum(emb * pull, axis=-1, keepdims=True)) * inv).astype(bf16)
    gproj[...] += lax.dot_general(low2, d_proj, TN, preferred_element_type=f32)
    d_h2 = lax.dot_general(d_proj, w_pr[...], NT, preferred_element_type=f32)
    d_res2 = norm_back(d_h2, n2, r2, gain2)
    d_ffn = d_res2.astype(bf16)
    dffn_ref[...] = d_ffn
    gvec[3:4, :] += jnp.sum(d_ffn.astype(f32), axis=0, keepdims=True)
    gvec[4:5, :] += jnp.sum(d_h2 * n2, axis=0, keepdims=True)
    gvec[5:6, :] += jnp.sum(d_h2, axis=0, keepdims=True)
    d_h1 = d_res2
    for j in range(FF // CHUNK):
        cols = slice(j * CHUNK, (j + 1) * CHUNK)
        d_act = lax.dot_general(d_ffn, w_dn[cols, :], NT, preferred_element_type=f32)
        d_pre = (slope[:, cols] * d_act).astype(bf16)
        dpre_ref[:, cols] = d_pre
        gup[:, cols] += jnp.sum(d_pre.astype(f32), axis=0, keepdims=True)
        d_h1 += lax.dot_general(d_pre, w_up[:, cols], NT, preferred_element_type=f32)
    d_res1 = norm_back(d_h1, n1, r1, gain1)
    res1_ref[...] = d_res1
    d_attn = d_res1.astype(bf16)
    dattn_ref[...] = d_attn
    gvec[0:1, :] += jnp.sum(d_attn.astype(f32), axis=0, keepdims=True)
    gvec[1:2, :] += jnp.sum(d_h1 * n1, axis=0, keepdims=True)
    gvec[2:3, :] += jnp.sum(d_h1, axis=0, keepdims=True)
    for d, out in enumerate((dc0, dc1, dc2, dc3)):
        out[...] = lax.dot_general(d_attn, heads_rows(d), NT, preferred_element_type=f32).astype(bf16)


def dense_kernel(n, fast, at_ref, *refs):
    ctx, tok, cot, vec, bias_up, refs = refs[:4], refs[4], refs[5], refs[6], refs[7], refs[8:]
    s, i = at_ref[0], at_ref[1]
    step = pl.program_id(0)
    own = D // n
    if not fast:
        w_o, w_up, w_dn, w_pr, refs = refs[0], refs[1], refs[2], refs[3], refs[4:]
        outs, (slope,) = refs[:-1], refs[-1:]
    else:
        a_refs, b_refs, refs = refs[:4], refs[4:8], refs[8:]
        outs, (slope, w_o, w_up, w_dn, w_pr) = refs[:-5], refs[-5:]

        @pl.when(step == 0)
        def _():
            core = s % 2
            for c in range(2):
                @pl.when(core == c)
                def _(c=c):
                    for at, ref in enumerate(a_refs):
                        cc = c if at < 2 else 1 - c
                        lanes = cc * (D // 2)
                        for p, diff in enumerate(held_order(n)):
                            j = i ^ (diff ^ (at % 2))
                            rows = pl.ds(pl.multiple_of(j * own, 32), own)
                            for b in range(FF // D):
                                w_up[rows, b * D + lanes:b * D + lanes + D // 2] = ref[p, b * own:(b + 1) * own, :]
                            base = (FF // D) * own
                            w_o[rows, lanes:lanes + D // 2] = ref[p, base:base + own, :]
                            base += own
                            for u in range(3):
                                part = own // 6
                                w_pr[pl.ds(pl.multiple_of(j * own + cc * (own // 2) + u * part, 16), part), :] = ref[p, base:base + part, u * EMB:(u + 1) * EMB]
            quarter = FF // n // 4
            for at, ref in enumerate(b_refs):
                for p, diff in enumerate(full_order(n)):
                    j = i ^ diff
                    w_dn[pl.ds(pl.multiple_of(j * (FF // n) + (s ^ at) * quarter, 32), quarter), :] = ref[p]
    dense_body(s, step, ctx, tok, cot, vec, bias_up, w_o, w_up, w_dn, w_pr, outs, slope)


def dense(n, at, ctx, tok, cot, vec, bias_up, weights, fast):
    rows = tok.shape[0]
    def by_rows(width):
        return pl.BlockSpec((BLK, width), lambda t, *_: (t, 0))
    one = pl.Buffered(1)
    ins = [by_rows(OWN)] * 4 + [by_rows(D), by_rows(EMB), whole(vec.shape), whole(bias_up.shape)]
    ins += [pl.BlockSpec(w.shape, lambda *_, nd=w.ndim: (0,) * nd, pipeline_mode=one) for w in weights]
    widths = [(EMB, f32), (D, f32), (FF, bf16), (FF, bf16), (D, bf16), (D, bf16), (D, bf16)] + [(OWN, bf16)] * 4
    outs = [by_rows(w) for w, _ in widths] + [whole((8, D)), whole((1, FF)), whole((D, EMB))]
    shapes = [jax.ShapeDtypeStruct((rows, w), t) for w, t in widths]
    shapes += [jax.ShapeDtypeStruct((8, D), f32), jax.ShapeDtypeStruct((1, FF), f32), jax.ShapeDtypeStruct((D, EMB), f32)]
    scratch = [pltpu.VMEM((BLK, FF), f32)]
    if fast:
        scratch += [pltpu.VMEM((D, D), bf16), pltpu.VMEM((D, FF), bf16), pltpu.VMEM((FF, D), bf16), pltpu.VMEM((D, EMB), bf16)]
    return pl.pallas_call(
        partial(dense_kernel, n, fast),
        grid_spec=pltpu.PrefetchScalarGridSpec(num_scalar_prefetch=1, grid=(rows // BLK,), in_specs=ins, out_specs=outs, scratch_shapes=scratch),
        out_shape=shapes, compiler_params=params(), cost_estimate=cost(40e9, 30e6), name="dense")(at, *ctx, tok, cot, vec, bias_up, *weights)


def fill_qkv(n, full, i, ins, w):
    own = D // n
    zero = jnp.zeros((D, LANES - OWN), bf16)
    for j in range(3):
        w[:, j * LANES + OWN:(j + 1) * LANES] = zero
    if full:
        for j in range(3):
            w[:, j * LANES:j * LANES + OWN] = ins[0][:, j * OWN:(j + 1) * OWN]
        return
    for extra, ref in enumerate(ins):
        for p, diff in enumerate(held_order(n)):
            rows = pl.ds(pl.multiple_of((i ^ (diff ^ extra)) * own, 32), own)
            for j in range(3):
                w[rows, j * LANES:j * LANES + OWN] = ref[p, :own, j * OWN:(j + 1) * OWN]


def share_kernel(n, full, at_ref, d_ref, *refs):
    ins, out_ref, w = refs[:-2], refs[-2], refs[-1]

    @pl.when(pl.program_id(0) == 0)
    def _():
        fill_qkv(n, full, at_ref[1], ins, w)
    out_ref[0] = lax.dot_general(d_ref[...], w[...], NT, preferred_element_type=f32).astype(bf16)


def by_piece(rows, width, diffs):
    def place(t, at):
        diff = diffs[0]
        for p in range(1, len(diffs)):
            diff = jnp.where(t == p, diffs[p], diff)
        return (at[0] ^ diff, 0)
    return pl.BlockSpec((rows, width), place)


def shares(n, at, d_qkv, weights, diffs):
    rows = d_qkv.shape[0] // 4
    return pl.pallas_call(
        partial(share_kernel, n, len(weights) == 1),
        grid_spec=pltpu.PrefetchScalarGridSpec(
            num_scalar_prefetch=1, grid=(len(diffs),), in_specs=[by_piece(rows, 3 * LANES, diffs)] + [whole(w.shape) for w in weights],
            out_specs=pl.BlockSpec((1, rows, D), lambda t, *_: (t, 0, 0)), scratch_shapes=[pltpu.VMEM((D, 3 * LANES), bf16)]),
        out_shape=jax.ShapeDtypeStruct((len(diffs), rows, D), bf16), compiler_params=params(),
        cost_estimate=cost(len(diffs) * rows * D * 3 * LANES * 4, 6e6), name="shares")(at, d_qkv, *weights)


def token_grad_kernel(n, at_ref, d_ref, x0, x1, x2, x3, out_ref, sum_ref, acc):
    t = pl.program_id(0)
    d = d_ref[...]
    total = jnp.sum(d.astype(f32), axis=0, keepdims=True)

    @pl.when(t == 0)
    def _():
        acc[...] = lax.dot_general(x0[...], d, TN, preferred_element_type=f32)
        sum_ref[...] = total
    for p, x in ((1, x1), (2, x2), (3, x3)):
        @pl.when(t == p)
        def _(x=x):
            acc[...] += lax.dot_general(x[...], d, TN, preferred_element_type=f32)
            sum_ref[...] += total

    @pl.when(t == 3)
    def _():
        own = D // n
        parts = []
        for h in range(HEADS):
            for j in range(3):
                parts.append(acc[:, j * LANES + h * HD:j * LANES + (h + 1) * HD])
        out_ref[...] = jnp.concatenate(parts, axis=1).astype(bf16)


def token_grad(n, at, d_qkv, xs):
    rows = xs[0].shape[0]
    return pl.pallas_call(
        partial(token_grad_kernel, n),
        grid_spec=pltpu.PrefetchScalarGridSpec(
            num_scalar_prefetch=1, grid=(4,), in_specs=[by_piece(rows, 3 * LANES, (0, 1, 2, 3))] + [whole(x.shape) for x in xs],
            out_specs=[whole((D, 3 * OWN)), whole((1, 3 * LANES))], scratch_shapes=[pltpu.VMEM((D, 3 * LANES), f32)]),
        out_shape=[jax.ShapeDtypeStruct((D, 3 * OWN), bf16), jax.ShapeDtypeStruct((1, 3 * LANES), f32)], compiler_params=params(),
        cost_estimate=cost(16e9, 10e6), name="token_grad")(at, d_qkv, *xs)


def swap(x, axis, mask, size):
    return lax.ppermute(x, axis, [(i, i ^ mask) for i in range(size)])


def tie(*xs):
    return lax.optimization_barrier(xs)


def pick(x, index, axis=0):
    return lax.dynamic_index_in_dim(x, index, axis, keepdims=False)


def lead_dot(left, right):
    return lax.dot_general(left, right, TN, preferred_element_type=f32)


def widen(held, m, n):
    return jnp.concatenate([held, swap(held, "dp", m, n)], axis=0)


def natural_blocks(x, n, i):
    order = full_order(n)
    table = jnp.asarray([order.index(k) for k in range(n)], jnp.int32)
    return jnp.stack([pick(x, table[j ^ i]) for j in range(n)])


def scatter_dp(part, n, i):
    held = part
    for m in masks(n):
        bit = (i // m) % 2
        held = held.reshape((held.shape[0] // 2, 2) + held.shape[1:])
        got = swap(pick(held, 1 - bit, 1), "dp", m, n)
        held = (pick(held, bit, 1).astype(f32) + got.astype(f32)).astype(bf16)
    return held[0]


def share_seq(held, c):
    got = swap(held, "seq", 2, 4)
    total = (held.astype(f32) + got.astype(f32)).astype(bf16)
    other = swap(total, "seq", 1, 4)
    first = jnp.where(c == 0, total, other)
    second = jnp.where(c == 0, other, total)
    return jnp.concatenate([first, second], axis=-1).astype(f32)


def shards(n, tokens, w_qkv, bias_query, bias_value, w_attn_out, bias_attn_out, norm1_gain, norm1_shift, w_up, bias_up,
           w_down, bias_down, norm2_gain, norm2_shift, w_proj, doc_ids, cotangent):
    s = lax.axis_index("seq")
    i = lax.axis_index("dp")
    c = s % 2
    own = D // n
    fast = own % 96 == 0
    steps = list(reversed(masks(n)))
    at = jnp.stack([s, i]).astype(jnp.int32)
    token_rows = tokens[0]
    doc_row = doc_ids[0]
    length = token_rows.shape[0]
    near = swap(token_rows, "seq", 1, 4)
    far = swap(token_rows, "seq", 2, 4)
    mine = lax.dynamic_slice_in_dim(w_qkv, s * 3 * OWN, 3 * OWN, 1)
    mine = mine.reshape(own, HEADS, 3, HD).transpose(0, 2, 1, 3).reshape(own, 3 * OWN)
    short = jnp.concatenate([bias_attn_out, norm1_gain, norm1_shift, bias_down, norm2_gain, norm2_shift, bias_query, bias_value, bias_up]).reshape(1, -1)
    width = short.shape[1]
    short = jnp.pad(short, ((0, 0), (0, -width % (3 * OWN)))).reshape(-1, 3 * OWN)
    early = jnp.concatenate([mine, short], axis=0)[None]
    for m in steps[:-1]:
        early = widen(early, m, n)
    early_got = swap(early, "dp", 1, n)
    opposite = swap(far, "seq", 1, 4)
    extra = jnp.concatenate([early[:, own:], early_got[:, own:]], axis=0).reshape(n, -1)
    order = jnp.asarray(full_order(n), jnp.int32)
    hot = (order[None, :] == (jnp.arange(n, dtype=jnp.int32) ^ i)[:, None]).astype(bf16)
    extra = jnp.dot(hot, extra, preferred_element_type=f32)
    vec = extra[:, :8 * own].reshape(n, 8, own).transpose(1, 0, 2).reshape(8, D)
    full_up_bias = extra[:, 8 * own:width].reshape(1, FF)
    quarter = FF // n // 4
    b = lax.dynamic_slice_in_dim(w_down, s * quarter, quarter, 0)[None]
    cols = [lax.dynamic_slice_in_dim(w_up, k * D + c * (D // 2), D // 2, 1) for k in range(FF // D)]
    cols.append(lax.dynamic_slice_in_dim(w_attn_out, c * (D // 2), D // 2, 1))
    if fast:
        half = lax.dynamic_slice_in_dim(w_proj, c * (own // 2), own // 2, 0)
        cols.append(jnp.concatenate([half[u * (own // 6):(u + 1) * (own // 6)] for u in range(3)], axis=1))
    a = jnp.concatenate(cols, axis=0)[None]
    b, _ = tie(b, early)
    for m in steps[:-1]:
        b = widen(b, m, n)
    a, _ = tie(a, b)
    b = widen(b, 1, n)
    for m in steps[:-1]:
        a = widen(a, m, n)
    a_got = swap(a, "dp", 1, n)
    lo, hi = block_ranges(doc_row)
    gap = jnp.zeros((1, LANES - OWN), f32)
    start = s * OWN
    bias_row = jnp.concatenate([
        lax.dynamic_slice(vec, (6, start), (1, OWN)), gap, jnp.zeros((1, LANES), f32), lax.dynamic_slice(vec, (7, start), (1, OWN)), gap], axis=1)
    doc_col = doc_row.reshape(-1, 1)
    if fast:
        heads_w = [early, early_got]
    else:
        heads_w = [natural_blocks(jnp.concatenate([early, early_got], axis=0)[:, :own], n, i).reshape(D, 3 * OWN)]
    qkv = project(n, at, [token_rows, near], (0, 1), heads_w, bias_row, doc_col)
    q, k, v = project(n, at, [far, opposite], (2, 3), heads_w, bias_row, doc_col, into=qkv)
    qa = None
    contexts, ctx = {}, {}
    for d in (2, 3, 1, 0):
        contexts[d], qa = attend_forward((s ^ d).reshape(1).astype(jnp.int32), lo, hi, q, k, v, into=qa)
        ctx[d] = swap(contexts[d], "seq", d, 4) if d else contexts[d]
    ctx = [ctx[d] for d in range(4)]
    contexts = [contexts[d] for d in range(4)]
    b_far = swap(b, "seq", 2, 4)
    b_near = swap(b, "seq", 1, 4)
    b_opposite = swap(b_far, "seq", 1, 4)
    a_other, a_got_other = swap(a, "seq", 1, 4), swap(a_got, "seq", 1, 4)
    if fast:
        weights = [a, a_got, a_other, a_got_other, b, b_near, b_far, b_opposite]
    else:
        mine_a = natural_blocks(jnp.concatenate([a, a_got], axis=0), n, i)
        other_a = natural_blocks(jnp.concatenate([a_other, a_got_other], axis=0), n, i)
        both = jnp.concatenate([jnp.where(c == 0, mine_a, other_a), jnp.where(c == 0, other_a, mine_a)], axis=2)
        up = jnp.concatenate([both[:, k * own:(k + 1) * own].reshape(D, D) for k in range(FF // D)], axis=1)
        all_b = jnp.stack([natural_blocks(x, n, i) for x in (b, b_near, b_far, b_opposite)])
        all_b = jnp.stack([pick(all_b, s ^ k) for k in range(4)], axis=1)
        proj = w_proj[None]
        for m in steps:
            proj = widen(proj, m, n)
        weights = [both[:, (FF // D) * own:].reshape(D, D), up, all_b.reshape(FF, D), natural_blocks(proj, n, i).reshape(D, EMB)]
    embed, d_res1, act, d_pre, h1, d_ffn, d_attn, dc0, dc1, dc2, dc3, gvec, gup, gproj = dense(
        n, at, ctx, token_rows, cotangent[0], vec, full_up_bias, weights, fast)
    d_contexts = [dc0] + [swap(x, "seq", d, 4) for d, x in ((1, dc1), (2, dc2), (3, dc3))]
    half_down = [lax.dynamic_slice_in_dim(d_ffn, x * (D // 2), D // 2, 1) for x in (c, 1 - c)]
    theirs = lead_dot(act, half_down[1]).astype(bf16).reshape(n, FF // n, D // 2)
    got_down = swap(theirs, "seq", 1, 4)
    mine_down = lead_dot(act, half_down[0]).reshape(n, FF // n, D // 2)
    pair_down = (mine_down + got_down.astype(f32)).astype(bf16)
    sum_down = share_seq(scatter_dp(pair_down, n, i), c)
    grad_up = lead_dot(h1, d_pre).astype(bf16).reshape(n, own, FF)
    grad_attn_out = jnp.concatenate([lead_dot(x, d_attn).astype(bf16)[None] for x in ctx], axis=0)
    grad_attn_out = jnp.stack([pick(grad_attn_out, s ^ j) for j in range(4)]).reshape(n, own, D)
    wide = grad_attn_out.reshape(n, 4, own // 4, D).transpose(0, 2, 1, 3).reshape(n, own // 4, FF)
    shorts = jnp.concatenate([gvec[k].reshape(n, own) for k in range(6)] + [gup.reshape(n, FF // n), gproj.reshape(n, own * EMB)], axis=1)
    used = shorts.shape[1]
    shorts = jnp.pad(shorts, ((0, 0), (0, -used % FF))).astype(bf16).reshape(n, -1, FF)
    bundle = jnp.concatenate([grad_up, wide, shorts], axis=1)
    half = FF // 2
    got_up = swap(lax.dynamic_slice_in_dim(bundle, (1 - c) * half, half, 2), "seq", 1, 4)
    pair_up = (lax.dynamic_slice_in_dim(bundle, c * half, half, 2).astype(f32) + got_up.astype(f32)).astype(bf16)
    sum_late = share_seq(scatter_dp(pair_up, n, i), c)
    sum_up = sum_late[:own]
    sum_attn_out = sum_late[own:own + own // 4].reshape(own // 4, 4, D).transpose(1, 0, 2).reshape(own, D)
    sums = sum_late[own + own // 4:].reshape(-1)
    d_qkv = attend_backward(at, lo, hi, qa, k, v, contexts, d_contexts)
    away = shares(n, at, d_qkv, heads_w, (3, 1))
    from_near = swap(away, "seq", 1, 4)
    home = shares(n, at, d_qkv, heads_w, (2, 0))
    pair = (home.astype(f32) + from_near.astype(f32)).astype(bf16)
    from_far = swap(pair[0], "seq", 2, 4)
    grad_input = d_res1 + pair[1].astype(f32) + from_far.astype(f32)
    grad_qkv, column_sums = token_grad(n, at, d_qkv, [token_rows, near, far, opposite])

    def spread(x):
        return lax.dynamic_update_slice_in_dim(jnp.zeros((D,), f32), x, start, 0).reshape(n, own)
    sides = jnp.concatenate([spread(column_sums[0, :OWN]), spread(column_sums[0, 2 * LANES:2 * LANES + OWN])], axis=1)
    sides = jnp.pad(sides, ((0, 0), (0, 3 * OWN - 2 * own))).astype(bf16).reshape(n, 1, 3 * OWN)
    tail = scatter_dp(jnp.concatenate([grad_qkv.reshape(n, own, 3 * OWN), sides], axis=1), n, i)
    two = jnp.stack([tail, swap(tail, "seq", 2, 4)])
    two_more = swap(two, "seq", 1, 4)
    x0, x1, x2, x3 = two[0], two_more[0], two[1], two_more[1]
    a0, a1, a2, a3 = jnp.where(c == 0, x0, x1), jnp.where(c == 0, x1, x0), jnp.where(c == 0, x2, x3), jnp.where(c == 0, x3, x2)
    low = s < 2
    parts = [jnp.where(low, a0, a2), jnp.where(low, a1, a3), jnp.where(low, a2, a0), jnp.where(low, a3, a1)]
    sum_qkv = jnp.concatenate([x[:own] for x in parts], axis=1).astype(f32)
    side_sum = sum(x[own].astype(f32) for x in parts)
    cut = 6 * own + FF // n
    return (
        embed[None],
        grad_input[None],
        sum_qkv,
        side_sum[:own],
        side_sum[own:2 * own],
        sum_attn_out,
        sums[:own],
        sums[own:2 * own],
        sums[2 * own:3 * own],
        sum_up,
        sums[6 * own:cut],
        sum_down,
        sums[3 * own:4 * own],
        sums[4 * own:5 * own],
        sums[5 * own:6 * own],
        sums[cut:used].reshape(own, EMB),
    )


def solution(mesh):
    rows, line, stream = P("dp", None), P("dp"), P("dp", "seq", None)
    in_specs = (stream, rows, line, line, rows, line, line, line, rows, line, rows, line, line, line, rows, rows, stream)
    out_specs = (stream, stream, rows, line, line, rows, line, line, line, rows, line, rows, line, line, line, rows)
    return jax.shard_map(partial(shards, mesh.shape["dp"]), mesh=mesh, in_specs=in_specs, out_specs=out_specs, check_vma=False)
```

time: 672 us -> 487 us (0.72)
  local copies, waits for them, and re-layouts: 130 us -> 47.5 us
  matrix products: 102 us -> 22.4 us
  Pallas kernels: 156 us -> 200 us
  waiting for transfers between devices: 170 us -> 136 us
  other arithmetic: 45.9 us -> 21.7 us
  between operations: 18.4 us -> 2.06 us
  starting transfers between devices: 42.2 us -> 53.4 us
    dot_general x12 -> x1, matrix products: 77.6 us -> 0.19 us  [shards(): extra = jnp.dot(hot, extra, preferred_element_type=f32)]
    pallas_call x3 -> x6, Pallas kernels: 27.5 us -> 77.3 us  [the longest x1 42.9 us: dense(): pl.pallas_call(partial(dense_kernel, n, fast), grid_spec=pltpu.PrefetchSc...]
    ppermute x45 -> x42, waiting for transfers between devices: 170 us -> 136 us  [swap(): return lax.ppermute(x, axis, [(i, i ^ mask) for i in range(size)])]
    dynamic_update_slice x14 -> x2, local copies, waits for them, and re-layouts: 25.3 us -> 0.39 us  [spread(): lax.dynamic_update_slice_in_dim(jnp.zeros((D,), f32), x, start, 0)]
    unnamed x148 -> x92, local copies, waits for them, and re-layouts: 31 us -> 14.7 us
    reshape x31 -> x15, local copies, waits for them, and re-layouts: 16.6 us -> 1.9 us  [the longest x1 0.7 us: shards(): sums[cut:used].reshape(own, EMB)]
    concatenate x11 -> x9, other arithmetic: 13.9 us -> 1.42 us  [the longest x1 0.88 us: shards(): bundle = jnp.concatenate([grad_up, wide, shorts], axis=1)]
    ppermute x45 -> x42, starting transfers between devices: 42.2 us -> 53.4 us  [swap(): return lax.ppermute(x, axis, [(i, i ^ mask) for i in range(size)])]
  transfers between devices with their start and end apart: 45 -> 42, of which waited for: 20 -> 18; matrix products, arithmetic and copies ran while one was open for 22% -> 15% of each run, Pallas kernels for 22% -> 33%
where the time goes in v2:
time: 487 us; the launch traced here: 483 us
  Pallas kernels  200 us (41%)
  waiting for transfers between devices  136 us (28%)
  starting transfers between devices  53.4 us (11%)
  local copies, waits for them, and re-layouts  47.5 us (10%)
  matrix products  22.4 us (5%)
  other arithmetic  21.7 us (4%)
    ppermute x42, waiting for transfers between devices, swap(): return lax.ppermute(x, axis, [(i, i ^ mask) for i in range(size)])  136 us
    pallas_call x1, Pallas kernels, attend_backward(): pl.pallas_call(backward_kernel, grid_spec=pltpu.PrefetchScalarGridSpec(nu...  70.4 us
    ppermute x42, starting transfers between devices, swap(): return lax.ppermute(x, axis, [(i, i ^ mask) for i in range(size)])  53.4 us
    pallas_call x4, Pallas kernels, attend_forward(): pl.pallas_call(forward_kernel, grid_spec=pltpu.PrefetchScalarGridSpec(num...  52.5 us
    pallas_call x1, Pallas kernels, dense(): pl.pallas_call(partial(dense_kernel, n, fast), grid_spec=pltpu.PrefetchSc...  42.9 us
    dot_general x7, matrix products, lead_dot(): return lax.dot_general(left, right, TN, preferred_element_type=f32)  22.2 us
    unnamed x92, local copies, waits for them, and re-layouts  14.7 us
    pallas_call x2, Pallas kernels, project(): pl.pallas_call(partial(project_kernel, n, len(xs), full), grid_spec=pltpu...  12.8 us
  transfers between devices with their start and end apart: 42, of which 18 were waited for; matrix products, arithmetic and copies ran while one was open for 15% of the time, Pallas kernels for 33%

profile of v2, /device:TPU:0, one launch (start us, length us, event | category | flops | bytes accessed | tf_op | source)
XLA Modules:
  0.0 482.9 jit_solution(2093881724559932830)
XLA Ops:
  5.2 6.1 %concatenate.74 = bf16[1152]{0:T(1024)(128)(2,1)S(1)} concatenate(bf16[96]{0:T(256)(128)(2,1)} %param.23, bf16[96]{0:T(256)(128)(2,1)} %param.24, bf16[96]{0:T(256)(128)(2,1)} %param.25, bf16[96]{0:T(256)(128)(2,1)} %param.29, bf16[96]{0:T(256)(128)(2,1)} %param.30, bf16[96]{0:T(256)(128)(2,1)} %param.31, bf16[96]{0:T(256)(128)(2,1)} %param.20, bf16[96]{0:T(256)(128)(2,1)} %param.21, ...), dimensions={0} | concatenate | bytes 4608 | tf_op jit(solution)/shard_map/concatenate | solution.py:613
  22.2 6.4 %collective-permute-done.3 = bf16[2,98,576]{2,1,0:T(8,128)(2,1)S(1)} collective-permute-done((bf16[2,98,576]{2,1,0:T(8,128)(2,1)S(1)}, bf16[2,98,576]{2,1,0:T(8,128)(2,1)S(1)}, u32[]{:S(2)}, u32[]{:S(2)}) %collective-permute-start.3) | collective-permute-done | bytes 225824 | tf_op jit(solution)/shard_map/ppermute | solution.py:553
  31.8 6.7 %collective-permute-done.9 = bf16[1,96,768]{2,1,0:T(8,128)(2,1)S(1)} collective-permute-done((bf16[1,96,768]{2,1,0:T(8,128)(2,1)S(1)}, bf16[1,96,768]{2,1,0:T(8,128)(2,1)S(1)}, u32[]{:S(2)}, u32[]{:S(2)}) %collective-permute-start.9) | collective-permute-done | bytes 147488 | tf_op jit(solution)/shard_map/ppermute | solution.py:553
  56.6 11.7 %collective-permute-done.11 = bf16[1,496,384]{2,1,0:T(8,128)(2,1)S(1)} collective-permute-done((bf16[1,496,384]{2,1,0:T(8,128)(2,1)S(1)}, bf16[1,496,384]{2,1,0:T(8,128)(2,1)S(1)}, u32[]{:S(2)}, u32[]{:S(2)}) %collective-permute-start.11) | collective-permute-done | bytes 380960 | tf_op jit(solution)/shard_map/ppermute | solution.py:553
  71.1 6.5 %project.2 = (bf16[3072,256]{1,0:T(8,128)(2,1)}, bf16[3072,256]{1,0:T(8,128)(2,1)}, bf16[3072,256]{1,0:T(8,128)(2,1)}) custom-call(s32[2]{0:T(128)} %pad_add_fusion.at_ref, bf16[768,768]{1,0:T(8,128)(2,1)} %bitcast.188, bf16[768,768]{1,0:T(8,128)(2,1)} %collective-permute-done.5.refs_1_.x1, bf16[4,98,576]{2,1,0:T(8,128)(2,1)} %copy-done.10, ...), custom_call_target="tpu_custom_call" | custom-call | flops 3623878656 | bytes 8000000 | tf_op jit(solution)/shard_map/project/pallas_call | solution.py:142
  78.9 7.6 %collective-permute-done.12 = bf16[2,496,384]{2,1,0:T(8,128)(2,1)} collective-permute-done((bf16[2,496,384]{2,1,0:T(8,128)(2,1)S(1)}, bf16[2,496,384]{2,1,0:T(8,128)(2,1)}, u32[]{:S(2)}, u32[]{:S(2)}) %collective-permute-start.12) | collective-permute-done | bytes 761888 | tf_op jit(solution)/shard_map/ppermute | solution.py:553
  90.1 6.2 %project.3 = (bf16[3072,256]{1,0:T(8,128)(2,1)}, bf16[3072,256]{1,0:T(8,128)(2,1)}, bf16[3072,256]{1,0:T(8,128)(2,1)}) custom-call(s32[2]{0:T(128)} %pad_add_fusion.at_ref, bf16[768,768]{1,0:T(8,128)(2,1)} %collective-permute-done.refs_0_.x2, ...), custom_call_target="tpu_custom_call", output_to_operand_aliasing={{0}: (7, {}), {1}: (8, {}), {2}: (9, {})} | custom-call | flops 3623878656 | bytes 8000000 | tf_op jit(solution)/shard_map/project/pallas_call | solution.py:142
  96.4 12.5 %attend_forward.4 = (bf16[768,192]{1,0:T(8,128)(2,1)}, bf16[3,3072,256]{2,1,0:T(8,128)(2,1)}) custom-call(s32[1]{0:T(128)} %bitcast.12.at_ref, s32[12]{0:T(128)} %get-tuple-element.122.lo_ref, s32[12]{0:T(128)} %get-tuple-element.121.hi_ref, bf16[3072,256]{1,0:T(8,128)(2,1)} %get-tuple-element.51.q_ref, bf16[3072,256]{1,0:T(8,128)(2,1)} %get-tuple-element.52.k_ref, ...), custom_call_target="tpu_custom_call" | custom-call | flops 8000000000 | bytes 8000000 | tf_op jit(solution)/shard_map/attend_forward/pallas_call | solution.py:217
  108.9 11.3 %attend_forward.5 = (bf16[768,192]{1,0:T(8,128)(2,1)}, bf16[3,3072,256]{2,1,0:T(8,128)(2,1)}) custom-call(s32[1]{0:T(128)} %bitcast.11.at_ref, s32[12]{0:T(128)} %get-tuple-element.122.lo_ref, s32[12]{0:T(128)} %get-tuple-element.121.hi_ref, bf16[3072,256]{1,0:T(8,128)(2,1)} %get-tuple-element.51.q_ref, ...), custom_call_target="tpu_custom_call", output_to_operand_aliasing={{1}: (6, {})} | custom-call | flops 8000000000 | bytes 8000000 | tf_op jit(solution)/shard_map/attend_forward/pallas_call | solution.py:217
  122.5 14.5 %attend_forward.6 = (bf16[768,192]{1,0:T(8,128)(2,1)}, bf16[3,3072,256]{2,1,0:T(8,128)(2,1)}) custom-call(s32[1]{0:T(128)} %bitcast.10.at_ref, s32[12]{0:T(128)} %get-tuple-element.122.lo_ref, s32[12]{0:T(128)} %get-tuple-element.121.hi_ref, bf16[3072,256]{1,0:T(8,128)(2,1)} %get-tuple-element.51.q_ref, ...), custom_call_target="tpu_custom_call", output_to_operand_aliasing={{1}: (6, {})} | custom-call | flops 8000000000 | bytes 8000000 | tf_op jit(solution)/shard_map/attend_forward/pallas_call | solution.py:217
  140.7 14.2 %attend_forward.7 = (bf16[768,192]{1,0:T(8,128)(2,1)}, bf16[3,3072,256]{2,1,0:T(8,128)(2,1)}) custom-call(s32[1]{0:T(128)} %bitcast.at_ref, s32[12]{0:T(128)} %get-tuple-element.122.lo_ref, s32[12]{0:T(128)} %get-tuple-element.121.hi_ref, bf16[3072,256]{1,0:T(8,128)(2,1)} %get-tuple-element.51.q_ref, ...), custom_call_target="tpu_custom_call", output_to_operand_aliasing={{1}: (6, {})} | custom-call | flops 8000000000 | bytes 8000000 | tf_op jit(solution)/shard_map/attend_forward/pallas_call | solution.py:217
  158.7 42.9 %dense.1 = (f32[768,128]{1,0:T(8,128)}, f32[768,768]{1,0:T(8,128)}, bf16[768,3072]{1,0:T(8,128)(2,1)}, bf16[768,3072]{1,0:T(8,128)(2,1)}, bf16[768,768]{1,0:T(8,...) custom-call(s32[2]{0:T(128)} %pad_add_fusion.at_ref, ...), custom_call_target="tpu_custom_call" | custom-call | flops 40000000000 | bytes 30000000 | tf_op jit(solution)/shard_map/dense/pallas_call | solution.py:465
  201.7 6.8 %convolution_convert_fusion.1 = bf16[3072,384]{1,0:T(8,128)(2,1)} fusion(bf16[768,3072]{1,0:T(8,128)(2,1)} %get-tuple-element.78, bf16[768,768]{1,0:T(8,128)(2,1)} %get-tuple-element.79, s32[]{:T(128)S(6)} %select_n.250), kind=kOutput, calls=%fused_computation.5 | convolution fusion | flops 1813118976 | bytes 7667716 | tf_op jit(solution)/shard_map/dot_general | solution.py:565
  215.6 6.6 %convolution_convert_fusion = bf16[768,3072]{1,0:T(8,128)(2,1)S(1)} fusion(bf16[768,768]{1,0:T(8,128)(2,1)} %get-tuple-element.72, bf16[768,3072]{1,0:T(8,128)(2,1)} %get-tuple-element.73), kind=kOutput, calls=%fused_computation.2 | convolution fusion | flops 3626237952 | bytes 10616832 | tf_op jit(solution)/shard_map/dot_general | solution.py:565
  233.9 70.4 %attend_backward.1.d_ref = bf16[3072,768]{1,0:T(8,128)(2,1)} custom-call(s32[2]{0:T(128)} %pad_add_fusion.at_ref, s32[12]{0:T(128)} %get-tuple-element.122.lo_ref, s32[12]{0:T(128)} %get-tuple-element.121.hi_ref, bf16[3,3072,256]{2,1,0:T(8,128)(2,1)} %get-tuple-element.65.qa_ref, bf16[3072,256]{1,0:T(8,128)(2,1)} %get-tuple-element.52.k_ref, ...), custom_call_target="tpu_custom_call" | custom-call | flops 60000002048 | bytes 16000000 | tf_op jit(solution)/shard_map/attend_backward/pallas_call | solution.py:297
  304.3 9.9 %token_grad.1 = (bf16[768,576]{1,0:T(8,128)(2,1)}, f32[1,768]{1,0:T(1,128)}) custom-call(s32[2]{0:T(128)} %pad_add_fusion.at_ref, bf16[3072,768]{1,0:T(8,128)(2,1)} %attend_backward.1.d_ref, bf16[768,768]{1,0:T(8,128)(2,1)} %bitcast.190, bf16[768,768]{1,0:T(8,128)(2,1)} %collective-permute-done.5.refs_1_.x1, ...), custom_call_target="tpu_custom_call" | custom-call | flops 16000000000 | bytes 10000000 | tf_op jit(solution)/shard_map/token_grad/pallas_call | solution.py:543
  318.2 7.1 %fusion.13 = f32[3072,384]{1,0:T(8,128)} fusion(bf16[768,3072]{1,0:T(8,128)(2,1)} %get-tuple-element.78, bf16[768,768]{1,0:T(8,128)(2,1)S(1)} %copy-done.36, s32[]{:T(128)S(6)} %select_n.216), kind=kOutput, calls=%fused_computation.45 | convolution fusion | flops 1811939328 | bytes 10027012 | tf_op jit(solution)/shard_map/dot_general | solution.py:565
  331.0 6.0 %shares.3 = bf16[2,768,768]{2,1,0:T(8,128)(2,1)} custom-call(s32[2]{0:T(128)} %pad_add_fusion.at_ref, bf16[3072,768]{1,0:T(8,128)(2,1)} %attend_backward.1.d_ref, bf16[4,98,576]{2,1,0:T(8,128)(2,1)} %copy-done.10, bf16[4,98,576]{2,1,0:T(8,128)(2,1)} %copy-done.11), custom_call_target="tpu_custom_call" | custom-call | flops 3623878656 | bytes 6000000 | tf_op jit(solution)/shard_map/shares/pallas_call | solution.py:507
  338.8 15.8 %collective-permute-start.27 = (bf16[1,97,576]{2,1,0:T(8,128)(2,1)S(1)}, bf16[1,97,576]{2,1,0:T(8,128)(2,1)S(1)}, u32[]{:S(2)}, u32[]{:S(2)}) collective-permute-start(bf16[1,97,576]{2,1,0:T(8,128)(2,1)S(1)} %constant_dynamic-slice_fusion.9), channel_id=1, source_target_pairs={{0,16},{4,20},{8,24},{12,28},{16,0},{20,4},{24,8},{28,12},{1,17},{... | collective-permute-start | bytes 335240 | tf_op jit(solution)/shard_map/ppermute | solution.py:553
  374.2 5.8 %shares.2 = bf16[2,768,768]{2,1,0:T(8,128)(2,1)} custom-call(s32[2]{0:T(128)} %pad_add_fusion.at_ref, bf16[3072,768]{1,0:T(8,128)(2,1)} %attend_backward.1.d_ref, bf16[4,98,576]{2,1,0:T(8,128)(2,1)} %copy-done.10, bf16[4,98,576]{2,1,0:T(8,128)(2,1)} %copy-done.11), custom_call_target="tpu_custom_call" | custom-call | flops 3623878656 | bytes 6000000 | tf_op jit(solution)/shard_map/shares/pallas_call | solution.py:507
  390.7 28.4 %collective-permute-done.31 = bf16[4,125,1536]{2,0,1:T(4,128)(2,1)} collective-permute-done((bf16[4,125,1536]{2,0,1:T(4,128)(2,1)}, bf16[4,125,1536]{2,0,1:T(4,128)(2,1)}, u32[]{:S(2)}, u32[]{:S(2)}) %collective-permute-start.31) | collective-permute-done | bytes 1536032 | tf_op jit(solution)/shard_map/ppermute | solution.py:553
  428.5 18.2 %collective-permute-done.32 = bf16[2,125,1536]{2,0,1:T(2,128)(2,1)S(1)} collective-permute-done((bf16[2,125,1536]{2,0,1:T(2,128)(2,1)S(1)}, bf16[2,125,1536]{2,0,1:T(2,128)(2,1)S(1)}, u32[]{:S(2)}, u32[]{:S(2)}) %collective-permute-start.32) | collective-permute-done | bytes 768032 | tf_op jit(solution)/shard_map/ppermute | solution.py:553
  449.2 16.0 %collective-permute-done.33 = bf16[1,125,1536]{2,1,0:T(8,128)(2,1)S(1)} collective-permute-done((bf16[1,125,1536]{2,1,0:T(8,128)(2,1)S(1)}, bf16[1,125,1536]{2,1,0:T(8,128)(2,1)S(1)}, u32[]{:S(2)}, u32[]{:S(2)}) %collective-permute-start.33) | collective-permute-done | bytes 384032 | tf_op jit(solution)/shard_map/ppermute | solution.py:553
  468.5 7.9 %collective-permute-done.34 = bf16[125,1536]{1,0:T(8,128)(2,1)S(1)} collective-permute-done((bf16[125,1536]{1,0:T(8,128)(2,1)S(1)}, bf16[125,1536]{1,0:T(8,128)(2,1)S(1)}, u32[]{:S(2)}, u32[]{:S(2)}) %collective-permute-start.34) | collective-permute-done | bytes 384032 | tf_op jit(solution)/shard_map/ppermute | solution.py:553
  (290 shorter events, 135.3 us)
Async XLA Ops:
  0.7 70.4 %collective-permute-start.5 = (bf16[768,768]{1,0:T(8,128)(2,1)}, bf16[768,768]{1,0:T(8,128)(2,1)}, u32[]{:S(2)}, u32[]{:S(2)}) collective-permute-start(bf16[768,768]{1,0:T(8,128)(2,1)} %bitcast.186), channel_id=1, source_target_pairs={{0,1},{1,0},{2,3},{3,2},{4,5},{5,4},{6,7},{7,6},{8,9},{9,8},{10,11... | collective-permute-start | bytes 3538952 | tf_op jit(solution)/shard_map/ppermute | solution.py:553
  1.2 55.2 %collective-permute-start = (bf16[768,768]{1,0:T(8,128)(2,1)}, bf16[768,768]{1,0:T(8,128)(2,1)}, u32[]{:S(2)}, u32[]{:S(2)}) collective-permute-start(bf16[768,768]{1,0:T(8,128)(2,1)} %bitcast.187), channel_id=1, source_target_pairs={{0,2},{1,3},{2,0},{3,1},{4,6},{5,7},{6,4},{7,5},{8,10},{9,11},{10,... | collective-permute-start | bytes 3538952 | tf_op jit(solution)/shard_map/ppermute | solution.py:553
  48.4 19.9 %collective-permute-start.11 = (bf16[1,496,384]{2,1,0:T(8,128)(2,1)S(1)}, bf16[1,496,384]{2,1,0:T(8,128)(2,1)S(1)}, u32[]{:S(2)}, u32[]{:S(2)}) collective-permute-start(bf16[1,496,384]{2,1,0:T(8,128)(2,1)S(1)} %bitcast.166), channel_id=1, source_target_pairs={{0,16},{4,20},{8,24},{12,28},{16,0},{20,4},{24,8},{28,12},{1,17},{... | collective-permute-start | bytes 1142792 | tf_op jit(solution)/shard_map/ppermute | solution.py:553
  53.9 23.7 %collective-permute-start.16 = (bf16[4,96,768]{2,1,0:T(8,128)(2,1)}, bf16[4,96,768]{2,1,0:T(8,128)(2,1)S(1)}, u32[]{:S(2)}, u32[]{:S(2)}) collective-permute-start(bf16[4,96,768]{2,1,0:T(8,128)(2,1)} %get-tuple-element.101), channel_id=1, source_target_pairs={{0,4},{4,0},{8,12},{12,8},{16,20},{20,16},{24,28},{28,24},{1,5},{5... | collective-permute-start | bytes 1769480 | tf_op jit(solution)/shard_map/ppermute | solution.py:553
  56.5 33.6 %collective-permute-start.1 = (bf16[768,768]{1,0:T(8,128)(2,1)}, bf16[768,768]{1,0:T(8,128)(2,1)}, u32[]{:S(2)}, u32[]{:S(2)}) collective-permute-start(bf16[768,768]{1,0:T(8,128)(2,1)} %collective-permute-done.refs_0_.x2), channel_id=1, source_target_pairs={{0,1},{1,0},{2,3},{3,2},{4,5},{5,4},{6,7},{7,6},{8,9},{9,8},{10,11... | collective-permute-start | bytes 3538952 | tf_op jit(solution)/shard_map/ppermute | solution.py:553
  78.5 41.7 %collective-permute-start.18 = (bf16[8,96,768]{2,1,0:T(8,128)(2,1)}, bf16[8,96,768]{2,1,0:T(8,128)(2,1)}, u32[]{:S(2)}, u32[]{:S(2)}) collective-permute-start(bf16[8,96,768]{2,1,0:T(8,128)(2,1)} %constant_dynamic-update-slice_fusion.7.refs_12_), channel_id=1, source_target_pairs={{0,2},{1,3},{2,0},{3,1},{4,6},{5,7},{6,4},{7,5},{8,10},{9,11},{10,... | collective-permute-start | bytes 3538952 | tf_op jit(solution)/shard_map/ppermute | solution.py:553
  78.9 59.0 %collective-permute-start.17 = (bf16[8,96,768]{2,1,0:T(8,128)(2,1)}, bf16[8,96,768]{2,1,0:T(8,128)(2,1)}, u32[]{:S(2)}, u32[]{:S(2)}) collective-permute-start(bf16[8,96,768]{2,1,0:T(8,128)(2,1)} %constant_dynamic-update-slice_fusion.7.refs_12_), channel_id=1, source_target_pairs={{0,1},{1,0},{2,3},{3,2},{4,5},{5,4},{6,7},{7,6},{8,9},{9,8},{10,11... | collective-permute-start | bytes 3538952 | tf_op jit(solution)/shard_map/ppermute | solution.py:553
  88.6 33.8 %collective-permute-start.13 = (bf16[4,496,384]{2,1,0:T(8,128)(2,1)}, bf16[4,496,384]{2,1,0:T(8,128)(2,1)}, u32[]{:S(2)}, u32[]{:S(2)}) collective-permute-start(bf16[4,496,384]{2,1,0:T(8,128)(2,1)} %constant_dynamic-update-slice_fusion.4.refs_8_), channel_id=1, source_target_pairs={{0,4},{4,0},{8,12},{12,8},{16,20},{20,16},{24,28},{28,24},{1,5},{5... | collective-permute-start | bytes 4571144 | tf_op jit(solution)/shard_map/ppermute | solution.py:553
  90.1 67.9 %collective-permute-start.14 = (bf16[4,496,384]{2,1,0:T(8,128)(2,1)}, bf16[4,496,384]{2,1,0:T(8,128)(2,1)}, u32[]{:S(2)}, u32[]{:S(2)}) collective-permute-start(bf16[4,496,384]{2,1,0:T(8,128)(2,1)} %constant_dynamic-update-slice_fusion.4.refs_8_), channel_id=1, source_target_pairs={{0,1},{1,0},{2,3},{3,2},{4,5},{5,4},{6,7},{7,6},{8,9},{9,8},{10,11... | collective-permute-start | bytes 4571144 | tf_op jit(solution)/shard_map/ppermute | solution.py:553
  120.2 37.8 %collective-permute-start.19 = (bf16[8,96,768]{2,1,0:T(8,128)(2,1)}, bf16[8,96,768]{2,1,0:T(8,128)(2,1)}, u32[]{:S(2)}, u32[]{:S(2)}) collective-permute-start(bf16[8,96,768]{2,1,0:T(8,128)(2,1)} %collective-permute-done.18.refs_14_), channel_id=1, source_target_pairs={{0,1},{1,0},{2,3},{3,2},{4,5},{5,4},{6,7},{7,6},{8,9},{9,8},{10,11... | collective-permute-start | bytes 3538952 | tf_op jit(solution)/shard_map/ppermute | solution.py:553
  122.5 35.5 %collective-permute-start.15 = (bf16[4,496,384]{2,1,0:T(8,128)(2,1)}, bf16[4,496,384]{2,1,0:T(8,128)(2,1)}, u32[]{:S(2)}, u32[]{:S(2)}) collective-permute-start(bf16[4,496,384]{2,1,0:T(8,128)(2,1)} %collective-permute-done.13.refs_9_), channel_id=1, source_target_pairs={{0,1},{1,0},{2,3},{3,2},{4,5},{5,4},{6,7},{7,6},{8,9},{9,8},{10,11... | collective-permute-start | bytes 4571144 | tf_op jit(solution)/shard_map/ppermute | solution.py:553
  139.4 18.6 %collective-permute-start.7 = (bf16[768,192]{1,0:T(8,128)(2,1)S(1)}, bf16[768,192]{1,0:T(8,128)(2,1)S(1)}, u32[]{:S(2)}, u32[]{:S(2)}) collective-permute-start(bf16[768,192]{1,0:T(8,128)(2,1)S(1)} %copy-done.28), channel_id=1, source_target_pairs={{0,2},{1,3},{2,0},{3,1},{4,6},{5,7},{6,4},{7,5},{8,10},{9,11},{10,... | collective-permute-start | bytes 884744 | tf_op jit(solution)/shard_map/ppermute | solution.py:553
  208.4 146.2 %collective-permute-start.36 = (bf16[8,384,384]{2,1,0:T(8,128)(2,1)}, bf16[8,384,384]{2,1,0:T(8,128)(2,1)}, u32[]{:S(2)}, u32[]{:S(2)}) collective-permute-start(bf16[8,384,384]{2,1,0:T(8,128)(2,1)} %bitcast.52), channel_id=1, source_target_pairs={{0,1},{1,0},{2,3},{3,2},{4,5},{5,4},{6,7},{7,6},{8,9},{9,8},{10,11... | collective-permute-start | bytes 7077896 | tf_op jit(solution)/shard_map/ppermute | solution.py:553
  229.1 131.8 %collective-permute-start.30 = (bf16[8,125,1536]{2,0,1:T(8,128)(2,1)}, bf16[8,125,1536]{2,0,1:T(8,128)(2,1)}, u32[]{:S(2)}, u32[]{:S(2)}) collective-permute-start(bf16[8,125,1536]{2,0,1:T(8,128)(2,1)} %copy.141), channel_id=1, source_target_pairs={{0,1},{1,0},{2,3},{3,2},{4,5},{5,4},{6,7},{7,6},{8,9},{9,8},{10,11... | collective-permute-start | bytes 9216008 | tf_op jit(solution)/shard_map/ppermute | solution.py:553
  337.0 86.8 %collective-permute-start.23 = (bf16[2,768,768]{2,1,0:T(8,128)(2,1)}, bf16[2,768,768]{2,1,0:T(8,128)(2,1)}, u32[]{:S(2)}, u32[]{:S(2)}) collective-permute-start(bf16[2,768,768]{2,1,0:T(8,128)(2,1)} %shares.3), channel_id=1, source_target_pairs={{0,1},{1,0},{2,3},{3,2},{4,5},{5,4},{6,7},{7,6},{8,9},{9,8},{10,11... | collective-permute-start | bytes 7077896 | tf_op jit(solution)/shard_map/ppermute | solution.py:553
  338.8 30.2 %collective-permute-start.27 = (bf16[1,97,576]{2,1,0:T(8,128)(2,1)S(1)}, bf16[1,97,576]{2,1,0:T(8,128)(2,1)S(1)}, u32[]{:S(2)}, u32[]{:S(2)}) collective-permute-start(bf16[1,97,576]{2,1,0:T(8,128)(2,1)S(1)} %constant_dynamic-slice_fusion.9), channel_id=1, source_target_pairs={{0,16},{4,20},{8,24},{12,28},{16,0},{20,4},{24,8},{28,12},{1,17},{... | collective-permute-start | bytes 335240 | tf_op jit(solution)/shard_map/ppermute | solution.py:553
  359.5 29.2 %collective-permute-start.37 = (bf16[4,384,384]{2,1,0:T(8,128)(2,1)}, bf16[4,384,384]{2,1,0:T(8,128)(2,1)}, u32[]{:S(2)}, u32[]{:S(2)}) collective-permute-start(bf16[4,384,384]{2,1,0:T(8,128)(2,1)} %dynamic-slice_bitcast_fusion.1), channel_id=1, source_target_pairs={{0,4},{4,0},{8,12},{12,8},{16,20},{20,16},{24,28},{28,24},{1,5},{5... | collective-permute-start | bytes 3538952 | tf_op jit(solution)/shard_map/ppermute | solution.py:553
  368.3 50.7 %collective-permute-start.31 = (bf16[4,125,1536]{2,0,1:T(4,128)(2,1)}, bf16[4,125,1536]{2,0,1:T(4,128)(2,1)}, u32[]{:S(2)}, u32[]{:S(2)}) collective-permute-start(bf16[4,125,1536]{2,0,1:T(4,128)(2,1)} %copy.143), channel_id=1, source_target_pairs={{0,4},{4,0},{8,12},{12,8},{16,20},{20,16},{24,28},{28,24},{1,5},{5... | collective-permute-start | bytes 4608008 | tf_op jit(solution)/shard_map/ppermute | solution.py:553
  390.3 37.6 %collective-permute-start.38 = (bf16[2,384,384]{2,1,0:T(8,128)(2,1)S(1)}, bf16[2,384,384]{2,1,0:T(8,128)(2,1)S(1)}, u32[]{:S(2)}, u32[]{:S(2)}) collective-permute-start(bf16[2,384,384]{2,1,0:T(8,128)(2,1)S(1)} %dynamic-slice_bitcast_fusion.3), channel_id=1, source_target_pairs={{0,8},{4,12},{8,0},{12,4},{16,24},{20,28},{24,16},{28,20},{1,9},{5... | collective-permute-start | bytes 1769480 | tf_op jit(solution)/shard_map/ppermute | solution.py:553
  421.7 25.0 %collective-permute-start.32 = (bf16[2,125,1536]{2,0,1:T(2,128)(2,1)S(1)}, bf16[2,125,1536]{2,0,1:T(2,128)(2,1)S(1)}, u32[]{:S(2)}, u32[]{:S(2)}) collective-permute-start(bf16[2,125,1536]{2,0,1:T(2,128)(2,1)S(1)} %copy.145), channel_id=1, source_target_pairs={{0,8},{4,12},{8,0},{12,4},{16,24},{20,28},{24,16},{28,20},{1,9},{5... | collective-permute-start | bytes 2304008 | tf_op jit(solution)/shard_map/ppermute | solution.py:553
  426.1 40.5 %collective-permute-start.24 = (bf16[768,768]{1,0:T(8,128)(2,1)S(1)}, bf16[768,768]{1,0:T(8,128)(2,1)S(1)}, u32[]{:S(2)}, u32[]{:S(2)}) collective-permute-start(bf16[768,768]{1,0:T(8,128)(2,1)S(1)} %slice_bitcast_fusion), channel_id=1, source_target_pairs={{0,2},{1,3},{2,0},{3,1},{4,6},{5,7},{6,4},{7,5},{8,10},{9,11},{10,... | collective-permute-start | bytes 3538952 | tf_op jit(solution)/shard_map/ppermute | solution.py:553
  428.1 19.5 %collective-permute-start.39 = (bf16[1,384,384]{2,1,0:T(8,128)(2,1)S(1)}, bf16[1,384,384]{2,1,0:T(8,128)(2,1)S(1)}, u32[]{:S(2)}, u32[]{:S(2)}) collective-permute-start(bf16[1,384,384]{2,1,0:T(8,128)(2,1)S(1)} %constant_dynamic-slice_fusion.2), channel_id=1, source_target_pairs={{0,16},{4,20},{8,24},{12,28},{16,0},{20,4},{24,8},{28,12},{1,17},{... | collective-permute-start | bytes 884744 | tf_op jit(solution)/shard_map/ppermute | solution.py:553
  446.9 18.3 %collective-permute-start.33 = (bf16[1,125,1536]{2,1,0:T(8,128)(2,1)S(1)}, bf16[1,125,1536]{2,1,0:T(8,128)(2,1)S(1)}, u32[]{:S(2)}, u32[]{:S(2)}) collective-permute-start(bf16[1,125,1536]{2,1,0:T(8,128)(2,1)S(1)} %constant_dynamic-slice_fusion.3), channel_id=1, source_target_pairs={{0,16},{4,20},{8,24},{12,28},{16,0},{20,4},{24,8},{28,12},{1,17},{... | collective-permute-start | bytes 1152008 | tf_op jit(solution)/shard_map/ppermute | solution.py:553
  447.7 20.7 %collective-permute-start.40 = (bf16[384,384]{1,0:T(8,128)(2,1)S(1)}, bf16[384,384]{1,0:T(8,128)(2,1)S(1)}, u32[]{:S(2)}, u32[]{:S(2)}) collective-permute-start(bf16[384,384]{1,0:T(8,128)(2,1)S(1)} %fusion.17), channel_id=1, source_target_pairs={{0,2},{1,3},{2,0},{3,1},{4,6},{5,7},{6,4},{7,5},{8,10},{9,11},{10,... | collective-permute-start | bytes 884744 | tf_op jit(solution)/shard_map/ppermute | solution.py:553
  (57 other events, 520.4 us)
